TPU v7x, 32 devices: a whole 2x2x4 slice. The times are simulated.
32 devices in a mesh: dp: 8 (over z, y), seq: 4 (over x, core).
Axes of the slice: x: 2, y: 2, z: 4, core: 2. Of those that a mesh axis runs over, the one named last changes fastest.
Arguments:
- tokens: bfloat16 [8, 1024, 1024], P('dp', 'seq'), may hold values from -6 to 6
- segments: int32 [8, 1024], P('dp'), may hold values from 0 to 1023, as said below
- valid_mask: int32 [8, 1024], P('dp'), may hold values from 0 to 1, as said below
- attention_gain: float32 [1024], P('dp'), may hold values from 0.25 to 1.75
- query_weight: float32 [1024, 1024], P('dp'), may hold values from -0.1875 to 0.1875
- key_weight: float32 [1024, 512], P('dp'), may hold values from -0.1875 to 0.1875
- value_weight: float32 [1024, 512], P('dp'), may hold values from -0.1875 to 0.1875
- query_gain: float32 [64], replicated, may hold values from 0.25 to 1.75
- key_gain: float32 [64], replicated, may hold values from 0.25 to 1.75
- output_weight: float32 [1024, 1024], P('dp'), may hold values from -0.5 to 0.5
- feedforward_gain: float32 [1024], P('dp'), may hold values from 0.25 to 1.75
- gate_weight: float32 [1024, 4608], P('dp'), may hold values from -0.1875 to 0.1875
- up_weight: float32 [1024, 4608], P('dp'), may hold values from -0.1875 to 0.1875
- down_weight: float32 [4608, 1024], P('dp'), may hold values from -0.09375 to 0.09375
- cotangent: bfloat16 [8, 1024, 1024], P('dp', 'seq'), may hold values from -6 to 6
Outputs:
- layer_out: bfloat16 [8, 1024, 1024], P('dp', 'seq')
- token_grad: bfloat16 [8, 1024, 1024], P('dp', 'seq')
- attention_gain_grad: float32 [1024], P(('dp', 'seq'))
- query_weight_grad: float32 [1024, 1024], P(('dp', 'seq'))
- key_weight_grad: float32 [1024, 512], P(('dp', 'seq'))
- value_weight_grad: float32 [1024, 512], P(('dp', 'seq'))
- query_gain_grad: float32 [64], replicated
- key_gain_grad: float32 [64], replicated
- output_weight_grad: float32 [1024, 1024], P(('dp', 'seq'))
- feedforward_gain_grad: float32 [1024], P(('dp', 'seq'))
- gate_weight_grad: float32 [1024, 4608], P(('dp', 'seq'))
- up_weight_grad: float32 [1024, 4608], P(('dp', 'seq'))
- down_weight_grad: float32 [4608, 1024], P(('dp', 'seq'))
Inputs may be any that keep to these rules, and one draw needn't show every extreme that they name: `segments`: document numbers start at 0 in each row and never fall; the row's last document is numbered 1024 - 1; every document but one has at most 128 tokens, and one document of exactly 512 tokens lies wholly among the row's valid tokens. `valid_mask`: each row is 1 on its first 1024 - k positions and 0 after them, for some k from 0 to 128.
All inputs are finite; a program needn't handle non-finite values.
Results may differ from a plain program's by a relative error of at most 0.017.
Values may be sent and summed in bfloat16 or wider, within the bound.
No kernel may reach another device: no remote copies, remote signals or barrier semaphores. Data moves between devices by JAX's collectives and lax.ppermute only.
A program may use at most 192 MiB of HBM per device.

v0:
```python
import functools
import math

import jax
import jax.numpy as jnp
from jax import lax
from jax.experimental import pallas as pl
from jax.experimental.pallas import tpu as pltpu
from jax.sharding import PartitionSpec as P

EPS = 1e-05
ROPE_BASE = 1000000.0
NEG_FILL = -1e30
BF = jnp.bfloat16
F32 = jnp.float32
BLOCK = 128
PAIR = 128
SEQ = 4
MEGA = 1024 * 1024


def dot(left, right, dims):
    return lax.dot_general(left, right, (dims, ((), ())), preferred_element_type=F32)


def mm(left, right):
    return dot(left, right, ((1,), (0,)))


def mm_nt(left, right):
    return dot(left, right, ((1,), (1,)))


def mm_tn(left, right):
    return dot(left, right, ((0,), (0,)))


def rms_stats(values):
    factor = lax.rsqrt(jnp.mean(values * values, axis=-1, keepdims=True) + EPS)
    return (values * factor, factor)


def rms_back(grad_unit, unit_values, factor):
    return factor * (
        grad_unit - unit_values * jnp.mean(grad_unit * unit_values, axis=-1, keepdims=True)
    )


def doc_positions(segment_row):
    length = segment_row.shape[0]
    places = jnp.arange(length, dtype=jnp.int32)
    change = jnp.concatenate([jnp.ones((1,), dtype=jnp.bool_), segment_row[1:] != segment_row[:-1]])
    starts = lax.cummax(jnp.where(change, places, jnp.zeros_like(places)), axis=0)
    return places - starts


def rope_tables(positions, head_dim):
    half = head_dim // 2
    lane = jnp.arange(PAIR, dtype=jnp.int32)
    frequency = ROPE_BASE ** (-(lane % half).astype(F32) / half)
    angles = positions.astype(F32)[:, None] * frequency[None, :]
    sign = jnp.where(lane % head_dim < half, -1.0, 1.0)
    return (jnp.cos(angles), jnp.sin(angles) * sign[None, :])


def whole_vmem(count):
    return [pl.BlockSpec(memory_space=pltpu.VMEM)] * count


def scalars(count):
    return [pl.BlockSpec(memory_space=pltpu.SMEM)] * count


def lanes(shape):
    return lax.broadcasted_iota(jnp.int32, shape, 1)


def head_means(values, head_dim):
    width = values.shape[1]
    row = lax.broadcasted_iota(jnp.int32, (width, width), 0) // head_dim
    column = lax.broadcasted_iota(jnp.int32, (width, width), 1) // head_dim
    spread = jnp.where(row == column, 1.0 / head_dim, 0.0).astype(BF)
    high = values.astype(BF)
    rest = (values - high.astype(F32)).astype(BF)
    return mm(high, spread) + mm(rest, spread)


def half_partner(values, head_dim):
    half = head_dim // 2
    width = values.shape[1]
    upper = (lanes(values.shape) % head_dim) >= half
    return jnp.where(
        upper, pltpu.roll(values, half, 1), pltpu.roll(values, width - half, 1)
    )


def stacked_heads(pair, head_dim):
    first = lanes(pair.shape) < head_dim
    zero = jnp.zeros_like(pair)
    return jnp.concatenate([jnp.where(first, pair, zero), jnp.where(first, zero, pair)], axis=0)


def side_by_side(stacked, head_dim):
    rows = stacked.shape[0] // 2
    return jnp.where(
        lanes((rows, stacked.shape[1])) < head_dim, stacked[:rows], stacked[rows:]
    )


def mask_bias(start_ref, usable_ref, first_row, first_key, rows, window):
    row = first_row + lax.broadcasted_iota(jnp.int32, (rows, window), 0)
    key = first_key + lax.broadcasted_iota(jnp.int32, (rows, window), 1)
    start = start_ref[pl.ds(first_row, rows), :]
    usable = usable_ref[:, pl.ds(first_key, window)] > 0
    allowed = ((key >= start) & (key <= row) & usable) | (key == row)
    bias = jnp.where(allowed, 0.0, NEG_FILL)
    return jnp.concatenate([bias, bias], axis=0)


def each_block(low_ref, row_length, body):
    long_window = min(5 * BLOCK, row_length)

    def step(index, carry):
        first_row = pl.multiple_of(index * BLOCK, BLOCK)
        short_key = jnp.maximum(first_row - BLOCK, 0)
        is_short = low_ref[index] >= short_key

        @pl.when(is_short)
        def _():
            body(first_row, pl.multiple_of(short_key, BLOCK), 2 * BLOCK)

        @pl.when(jnp.logical_not(is_short))
        def _():
            long_key = jnp.maximum(first_row + BLOCK - long_window, 0)
            body(first_row, pl.multiple_of(long_key, BLOCK), long_window)

        return carry

    lax.fori_loop(0, row_length // BLOCK, step, 0)


def load_pieces(offset_ref, piece_refs, semaphore, *targets):
    copies = []
    for index, piece in enumerate(piece_refs):
        start = pl.multiple_of(offset_ref[index], 16)
        for part, (target, column) in enumerate(targets):
            rows = pl.ds(start, piece.shape[0])
            copies.append(
                pltpu.make_async_copy(
                    piece.at[:, column : column + target.shape[1]],
                    target.at[rows, :],
                    semaphore.at[part, index],
                )
            )
    for copy in copies:
        copy.start()

    def wait():
        for copy in copies:
            copy.wait()

    return wait


def columns_kernel(column, offset_ref, *rest):
    (*piece_refs, out_ref, semaphore) = rest
    load_pieces(offset_ref, piece_refs, semaphore, (out_ref, column))()


def project_kernel(
    head_dim,
    place_ref,
    offset_ref,
    x0_ref,
    x1_ref,
    x2_ref,
    x3_ref,
    cos_ref,
    sin_ref,
    gain_ref,
    *rest,
):
    (*piece_refs, unit_ref, raw_ref, query_ref, key_ref, value_ref, weight_ref) = rest[:-1]
    semaphore = rest[-1]
    wait = load_pieces(offset_ref, piece_refs, semaphore, (weight_ref, 0))
    place = place_ref[0]
    rows_each = x0_ref.shape[0]
    row_length = unit_ref.shape[0]
    query_groups = query_ref.shape[1] // PAIR
    for index, piece in enumerate((x0_ref, x1_ref, x2_ref, x3_ref)):

        def normalize(step, carry, piece=piece, base=(place ^ index) * rows_each):
            start = pl.multiple_of(step * BLOCK, BLOCK)
            values = piece[pl.ds(start, BLOCK), :].astype(F32)
            factor = lax.rsqrt(jnp.mean(values * values, axis=-1, keepdims=True) + EPS)
            rows = pl.ds(pl.multiple_of(base + start, BLOCK), BLOCK)
            unit_ref[rows, :] = (values * factor).astype(BF)
            return carry

        lax.fori_loop(0, rows_each // BLOCK, normalize, 0)
    wait()

    def project(step, carry):
        rows = pl.ds(pl.multiple_of(step * rows_each, rows_each), rows_each)
        raw = mm(unit_ref[rows, :], weight_ref[...])
        raw_ref[rows, :] = raw[:, : raw_ref.shape[1]]
        cos = cos_ref[rows, :]
        sin = sin_ref[rows, :]
        for group in range(query_groups + 1):
            is_key = group == query_groups
            values = raw[:, group * PAIR : (group + 1) * PAIR]
            factor = lax.rsqrt(head_means(values * values, head_dim) + EPS)
            scaled = values * factor * gain_ref[int(is_key) : int(is_key) + 1, :]
            turned = scaled * cos + half_partner(scaled, head_dim) * sin
            if is_key:
                crossed = pltpu.roll(turned, head_dim, 1)
                first = lanes(turned.shape) < head_dim
                key_ref[rows, :PAIR] = jnp.where(first, turned, crossed).astype(BF)
                key_ref[rows, PAIR:] = jnp.where(first, crossed, turned).astype(BF)
                values = raw[:, (group + 1) * PAIR :]
                crossed = pltpu.roll(values, head_dim, 1)
                value_ref[rows, :PAIR] = jnp.where(first, values, crossed).astype(BF)
                value_ref[rows, PAIR:] = jnp.where(first, crossed, values).astype(BF)
            else:
                query_ref[rows, group * PAIR : (group + 1) * PAIR] = (
                    turned * (1.0 / math.sqrt(head_dim))
                ).astype(BF)
        return carry

    lax.fori_loop(0, row_length // rows_each, project, 0)


def attend_kernel(
    head_dim, low_ref, query_ref, key_ref, value_ref, start_ref, usable_ref, mixed_ref
):
    row_length = query_ref.shape[0]
    query_groups = query_ref.shape[1] // PAIR

    def attend(first_row, first_key, window):
        bias = mask_bias(start_ref, usable_ref, first_row, first_key, BLOCK, window)
        rows = pl.ds(first_row, BLOCK)
        keys = pl.ds(first_key, window)
        found = []
        for group in range(query_groups):
            pair = slice(group * PAIR, (group + 1) * PAIR)
            stacked = stacked_heads(query_ref[rows, pair], head_dim)
            grown = jnp.exp(mm_nt(stacked, key_ref[keys, pair]) + bias)
            mixed = mm(grown.astype(BF), value_ref[keys, pair])
            mixed = mixed * (1.0 / jnp.sum(grown, axis=-1, keepdims=True))
            found.append(side_by_side(mixed, head_dim).astype(BF))
        mixed_ref[rows, :] = jnp.concatenate(found, axis=1)

    each_block(low_ref, row_length, attend)


def middle_kernel(
    place_ref,
    x0_ref,
    x1_ref,
    x2_ref,
    x3_ref,
    o0_ref,
    o1_ref,
    o2_ref,
    o3_ref,
    w0_ref,
    w1_ref,
    w2_ref,
    w3_ref,
    unit_ref,
    here_ref,
    sum_ref,
):
    place = place_ref[0]
    rows_each, width = x0_ref.shape
    heads = o0_ref.shape[1]
    columns = w0_ref.shape[1]
    for index, piece in enumerate((x0_ref, x1_ref, x2_ref, x3_ref)):
        base = pl.multiple_of((place ^ index) * rows_each, rows_each)
        rows = pl.ds(base, rows_each)
        for part, weight in enumerate((w0_ref, w1_ref, w2_ref, w3_ref)):
            total = None
            for other, mixed in enumerate((o0_ref, o1_ref, o2_ref, o3_ref)):
                features = pl.ds(pl.multiple_of((place ^ other) * heads, heads), heads)
                term = mm(mixed[rows, :], weight[features, :])
                total = term if total is None else total + term
            spot = pl.multiple_of((place ^ part) * columns, columns)
            sum_ref[:, pl.ds(spot, columns)] = total


        def normalize(step, carry, piece=piece, index=index):
            start = pl.multiple_of(step * BLOCK, BLOCK)
            part = pl.ds(start, BLOCK)
            values = sum_ref[part, :] + piece[part, :].astype(F32)
            if index == 0:
                here_ref[part, :] = values
            factor = lax.rsqrt(jnp.mean(values * values, axis=-1, keepdims=True) + EPS)
            target = pl.ds(pl.multiple_of(index * rows_each + start, BLOCK), BLOCK)
            unit_ref[target, :] = (values * factor).astype(BF)
            return carry

        lax.fori_loop(0, rows_each // BLOCK, normalize, 0)


def hidden_kernel(offset_ref, unit_ref, *rest):
    (*piece_refs, hidden_ref, gate_factor_ref, up_factor_ref, weight_ref, semaphore) = rest
    here = hidden_ref.shape[1]

    @pl.when(pl.program_id(0) == 0)
    def _():
        load_pieces(offset_ref, piece_refs, semaphore, (weight_ref, 0))()

    both = mm(unit_ref[...], weight_ref[...])
    gate = both[:, :here]
    up = both[:, here:]
    sig = 1.0 / (1.0 + jnp.exp(-gate))
    silu = gate * sig
    hidden_ref[...] = (silu * up).astype(BF)
    gate_factor_ref[...] = (up * sig * (1.0 + gate * (1.0 - sig))).astype(BF)
    up_factor_ref[...] = silu.astype(BF)


def hidden_grad_kernel(offset_ref, grad_ref, gate_factor_ref, up_factor_ref, *rest):
    (*piece_refs, both_ref, down_ref, semaphore) = rest
    here = gate_factor_ref.shape[1]

    @pl.when(pl.program_id(0) == 0)
    def _():
        load_pieces(offset_ref, piece_refs, semaphore, (down_ref, 0))()

    grad = mm_nt(grad_ref[...], down_ref[...])
    both_ref[:, :here] = (grad * gate_factor_ref[...].astype(F32)).astype(BF)
    both_ref[:, here:] = (grad * up_factor_ref[...].astype(F32)).astype(BF)


def split_kernel(transposed, order_ref, offset_ref, left_ref, *rest):
    (*piece_refs, keep_ref, send_ref, right_ref, semaphore) = rest

    @pl.when(pl.program_id(0) == 0)
    def _():
        load_pieces(offset_ref, piece_refs, semaphore, (right_ref, 0))()

    product = (mm_nt if transposed else mm)(left_ref[...], right_ref[...])

    @pl.when(pl.program_id(0) % 2 == 0)
    def _():
        keep_ref[...] = product

    @pl.when(pl.program_id(0) % 2 == 1)
    def _():
        send_ref[...] = product.astype(BF)


def output_grad_kernel(
    chunk_rows,
    place_ref,
    g0_ref,
    g1_ref,
    g2_ref,
    g3_ref,
    mixed_ref,
    w0_ref,
    w1_ref,
    w2_ref,
    w3_ref,
    grad_ref,
    terms_ref,
    total_ref,
):
    place = place_ref[0]
    rows_each = g0_ref.shape[0]
    heads = mixed_ref.shape[1]
    columns = w0_ref.shape[1]
    features = pl.ds(pl.multiple_of(place * heads, heads), heads)
    for index, grads in enumerate((g0_ref, g1_ref, g2_ref, g3_ref)):
        rows = pl.ds(pl.multiple_of((place ^ index) * rows_each, rows_each), rows_each)
        total = None
        for part, weight in enumerate((w0_ref, w1_ref, w2_ref, w3_ref)):
            spot = pl.ds(pl.multiple_of((place ^ part) * columns, columns), columns)
            term = mm_nt(grads[:, spot], weight[features, :])
            total = term if total is None else total + term
        grad_ref[rows, :] = total.astype(BF)
        term = mm_tn(mixed_ref[rows, :], grads[...])
        total_ref[...] = term if index == 0 else total_ref[...] + term
    sides = total_ref.shape[1] // terms_ref.shape[1]
    width = terms_ref.shape[1]
    chunks = terms_ref.shape[0] // sides // chunk_rows
    for step in range(chunks):
        for side in range(sides):
            start = (step * sides + side) * chunk_rows
            terms_ref[start : start + chunk_rows, :] = total_ref[
                step * chunk_rows : (step + 1) * chunk_rows, side * width : (side + 1) * width
            ]


def back_kernel(
    head_dim,
    low_ref,
    grad_ref,
    query_ref,
    key_ref,
    value_ref,
    raw_ref,
    cos_ref,
    sin_ref,
    gain_ref,
    start_ref,
    usable_ref,
    out_ref,
    terms_ref,
    key_sum_ref,
    value_sum_ref,
):
    row_length = grad_ref.shape[0]
    query_groups = query_ref.shape[1] // PAIR
    scale = 1.0 / math.sqrt(head_dim)
    key_sum_ref[...] = jnp.zeros_like(key_sum_ref)
    value_sum_ref[...] = jnp.zeros_like(value_sum_ref)
    terms_ref[...] = jnp.zeros_like(terms_ref)

    def through_norm(rows, group, grad, kind):
        grad = grad.astype(BF).astype(F32)
        turned = grad * cos_ref[rows, :] - half_partner(grad, head_dim) * sin_ref[rows, :]
        values = raw_ref[rows, group * PAIR : (group + 1) * PAIR]
        factor = lax.rsqrt(head_means(values * values, head_dim) + EPS)
        unit = values * factor
        terms_ref[kind : kind + 1, :] += jnp.sum(turned * unit, axis=0, keepdims=True)
        scaled = turned * gain_ref[kind : kind + 1, :]
        back = factor * (scaled - unit * head_means(scaled * unit, head_dim))
        out_ref[rows, group * PAIR : (group + 1) * PAIR] = back.astype(BF)

    def attend(first_row, first_key, window):
        bias = mask_bias(start_ref, usable_ref, first_row, first_key, BLOCK, window)
        rows = pl.ds(first_row, BLOCK)
        keys = pl.ds(first_key, window)
        found = []
        for group in range(query_groups):
            pair = slice(group * PAIR, (group + 1) * PAIR)
            stacked = stacked_heads(query_ref[rows, pair], head_dim)
            grads = stacked_heads(grad_ref[rows, pair], head_dim)
            grown = jnp.exp(mm_nt(stacked, key_ref[keys, pair]) + bias)
            share = grown * (1.0 / jnp.sum(grown, axis=-1, keepdims=True))
            grad_share = mm_nt(grads, value_ref[keys, pair])
            centre = jnp.sum(share * grad_share, axis=-1, keepdims=True)
            grad_score = (share * (grad_share - centre)).astype(BF)
            grad_query = side_by_side(mm(grad_score, key_ref[keys, pair]), head_dim) * scale
            key_term = mm_tn(grad_score, stacked)
            found.append((grad_query, key_term, mm_tn(share.astype(BF), grads)))
        for group, (grad_query, key_term, value_term) in enumerate(found):
            pair = slice(group * PAIR, (group + 1) * PAIR)
            key_sum_ref[keys, pair] += key_term
            value_sum_ref[keys, pair] += value_term
            through_norm(rows, group, grad_query, 0)

    each_block(low_ref, row_length, attend)

    def folded(sum_ref, rows):
        first = sum_ref[rows, :PAIR]
        second = sum_ref[rows, PAIR:]
        return jnp.where(
            lanes(first.shape) < head_dim,
            first + pltpu.roll(first, head_dim, 1),
            second + pltpu.roll(second, head_dim, 1),
        )

    def finish(step, carry):
        rows = pl.ds(pl.multiple_of(step * BLOCK, BLOCK), BLOCK)
        through_norm(rows, query_groups, folded(key_sum_ref, rows), 1)
        out_ref[rows, (query_groups + 1) * PAIR :] = folded(value_sum_ref, rows).astype(BF)
        return carry

    lax.fori_loop(0, row_length // BLOCK, finish, 0)


def attention_pack_kernel(
    place_ref,
    gain_ref,
    query_ref,
    key_ref,
    value_ref,
    output_ref,
    pack_ref,
    wide_ref,
    semaphore,
):
    gain = gain_ref[...].astype(BF).astype(F32)
    weights = (query_ref, key_ref, value_ref, output_ref)
    start = 0
    copies = []
    for index, weight_ref in enumerate(weights):
        size = weight_ref.shape[1] // SEQ
        column = pl.multiple_of(place_ref[0] * size, size)
        copies.append(
            pltpu.make_async_copy(
                weight_ref.at[:, pl.ds(column, size)],
                wide_ref.at[:, start : start + size],
                semaphore.at[index],
            )
        )
        copies[-1].start()
        start += size
    start = 0
    for index, weight_ref in enumerate(weights):
        size = weight_ref.shape[1] // SEQ
        copies[index].wait()
        values = wide_ref[:, start : start + size].astype(BF)
        if index < len(weights) - 1:
            values = (values.astype(F32) * gain).astype(BF)
        pack_ref[:, start : start + size] = values
        start += size


def hidden_pack_kernel(
    pieces, place_ref, gain_ref, gate_ref, up_ref, pack_ref, wide_ref, semaphore
):
    piece = gate_ref.shape[1] // (pieces * SEQ)
    here = pieces * piece
    chunk = 32
    steps = gate_ref.shape[0] // chunk
    weights = (gate_ref, up_ref)

    def copy(index, part):
        rows = pl.ds(pl.multiple_of(index * chunk, chunk), chunk)
        return pltpu.make_async_copy(
            weights[part].at[rows, :], wide_ref.at[part, rows, :], semaphore.at[part, index]
        )

    for index in range(steps):
        for part in range(2):
            copy(index, part).start()
    for place in range(SEQ):

        @pl.when(place_ref[0] == place)
        def _(place=place):
            def step(index, carry):
                rows = pl.ds(pl.multiple_of(index * chunk, chunk), chunk)
                gain = gain_ref[rows, :].astype(BF).astype(F32)
                for part in range(2):
                    copy(index, part).wait()
                    joined = jnp.concatenate(
                        [
                            wide_ref[part, rows, start : start + piece]
                            for start in range(place * piece, gate_ref.shape[1], SEQ * piece)
                        ],
                        axis=1,
                    )
                    pack_ref[rows, part * here : (part + 1) * here] = (
                        joined.astype(BF).astype(F32) * gain
                    ).astype(BF)
                return carry

            lax.fori_loop(0, steps, step, 0)


def hidden_owner_kernel(
    pieces, place_ref, sums_ref, gate_ref, up_ref, gain_ref, gate_grad_ref, up_grad_ref, terms_ref
):
    seq_count = sums_ref.shape[0]
    here = sums_ref.shape[2] // 2
    piece = here // pieces
    gain = gain_ref[...].astype(BF).astype(F32)
    total = None
    for part, (weight_ref, grad_ref) in enumerate(
        ((gate_ref, gate_grad_ref), (up_ref, up_grad_ref))
    ):
        sums = [sums_ref[seq].astype(F32) for seq in range(seq_count)]
        joined = jnp.concatenate(
            [
                sums[seq][:, part * here + step * piece : part * here + (step + 1) * piece]
                for step in range(pieces)
                for seq in range(seq_count)
            ],
            axis=1,
        )
        term = row_sums(weight_ref[...].astype(BF).astype(F32) * joined)
        total = term if total is None else total + term
        grad_ref[...] = joined * gain
    terms_ref[...] = total


def attention_owner_kernel(
    place_ref,
    s0_ref,
    s1_ref,
    s2_ref,
    s3_ref,
    query_ref,
    key_ref,
    value_ref,
    gain_ref,
    query_grad_ref,
    key_grad_ref,
    value_grad_ref,
    terms_ref,
):
    place = place_ref[0]
    gain = gain_ref[...].astype(BF).astype(F32)
    pieces = (s0_ref, s1_ref, s2_ref, s3_ref)
    rows = query_ref.shape[0]
    start = 0
    total = None
    for weight_ref, grad_ref in (
        (query_ref, query_grad_ref),
        (key_ref, key_grad_ref),
        (value_ref, value_grad_ref),
    ):
        size = weight_ref.shape[1] // len(pieces)
        for index, sums in enumerate(pieces):
            columns = pl.ds(pl.multiple_of((place ^ index) * size, size), size)
            values = sums[:rows, start : start + size].astype(F32)
            weight = weight_ref[:, columns].astype(BF).astype(F32)
            term = row_sums(weight * values)
            total = term if total is None else total + term
            grad_ref[:, columns] = values * gain
        start += size
    terms_ref[...] = total


def row_sums(values):
    ones = jnp.ones((8, values.shape[1]), BF)
    high = values.astype(BF)
    rest = (values - high.astype(F32)).astype(BF)
    return (mm_nt(ones, high) + mm_nt(ones, rest))[:1]


def placed_call(kernel, results, place_array, operands, blocks, vmem, flops=0, moved=0):
    return pl.pallas_call(
        kernel,
        out_shape=[jax.ShapeDtypeStruct(shape, kind) for shape, kind in results],
        grid_spec=pltpu.PrefetchScalarGridSpec(
            num_scalar_prefetch=1,
            grid=(1,),
            in_specs=[pl.BlockSpec(shape, index) for shape, index in blocks],
            out_specs=[
                pl.BlockSpec(shape, lambda i, place, rank=len(shape): (0,) * rank)
                for shape, _ in results
            ],
        ),
        compiler_params=pltpu.CompilerParams(vmem_limit_bytes=vmem * MEGA),
        cost_estimate=cost(kernel, flops),
    )(place_array, *operands)


def own_rows_block(i, place):
    return (place[0], 0)


def everything(i, place):
    return (0, 0)


MICROSECONDS = {
    "attention_pack_kernel": 2.6,
    "hidden_pack_kernel": 4.2,
    "columns_kernel": 2.6,
    "project_kernel": 9.5,
    "attend_kernel": 7.0,
    "middle_kernel": 5.0,
    "hidden_kernel": 9.0,
    "hidden_grad_kernel": 5.4,
    "output_grad_kernel": 3.0,
    "back_kernel": 15.6,
    "hidden_owner_kernel": 3.1,
    "attention_owner_kernel": 1.9,
}


def cost(kernel, flops):
    name = getattr(kernel, "func", kernel).__name__
    time = MICROSECONDS.get(name, flops * 2.0e-9 + 0.5) * 0.5
    return pl.CostEstimate(flops=int(time * 1.15e9), bytes_accessed=0, transcendentals=0)


def call(
    kernel, results, scalar_count, operands, vmem, pieces=(), scratch=(), flops=0, moved=0
):
    return pl.pallas_call(
        kernel,
        out_shape=[jax.ShapeDtypeStruct(shape, kind) for shape, kind in results],
        in_specs=scalars(scalar_count)
        + whole_vmem(len(operands) - scalar_count)
        + [pl.BlockSpec(memory_space=pltpu.HBM)] * len(pieces),
        out_specs=whole_vmem(len(results)),
        scratch_shapes=list(scratch),
        compiler_params=pltpu.CompilerParams(vmem_limit_bytes=vmem * MEGA),
        cost_estimate=cost(kernel, flops),
    )(*operands, *pieces)


def block_call(kernel, results, scalar_arrays, operands, vmem, pieces, scratch, flops, moved):
    return pl.pallas_call(
        kernel,
        out_shape=[jax.ShapeDtypeStruct(shape, kind) for shape, kind, _, _ in results],
        grid_spec=pltpu.PrefetchScalarGridSpec(
            num_scalar_prefetch=len(scalar_arrays),
            grid=(4,),
            in_specs=[pl.BlockSpec(shape, index) for _, shape, index in operands]
            + [pl.BlockSpec(memory_space=pltpu.HBM)] * len(pieces),
            out_specs=[pl.BlockSpec(shape, index) for _, _, shape, index in results],
            scratch_shapes=list(scratch),
        ),
        compiler_params=pltpu.CompilerParams(vmem_limit_bytes=vmem * MEGA),
        cost_estimate=cost(kernel, flops),
    )(*scalar_arrays, *(array for array, _, _ in operands), *pieces)


def row_block(step, *scalar_refs):
    return (step, 0)


def half_block(step, *scalar_refs):
    return (step // 2, 0)


def first_block(step, *scalar_refs):
    return (0, 0)


def ordered_block(step, order_ref, *scalar_refs):
    return (order_ref[step], 0)


def split_product(left, right_shape, offsets, pieces, transposed, order):
    rows = left.shape[0] // 4
    width = right_shape[0] if transposed else right_shape[1]
    return block_call(
        functools.partial(split_kernel, transposed),
        [
            ((2 * rows, width), F32, (rows, width), half_block),
            ((2 * rows, width), BF, (rows, width), half_block),
        ],
        (order, offsets),
        [(left, (rows, left.shape[1]), ordered_block)],
        20,
        pieces,
        [pltpu.VMEM(right_shape, BF), pltpu.SemaphoreType.DMA((1, len(pieces)))],
        2 * left.shape[0] * left.shape[1] * width,
        2 * (left.size + right_shape[0] * right_shape[1]) + 6 * left.shape[0] * width,
    )


def swap(values, bit):
    count = lax.axis_size("seq")
    return lax.ppermute(values, "seq", [(i, i ^ bit) for i in range(count)])


def seq_pieces(values):
    far = swap(values, 2)
    near = swap(values, 1)
    return (values, near, far, swap(far, 1))


def after(values, *others):
    return lax.optimization_barrier((values, others))[0]


def ring_length():
    count = lax.axis_size("dp")
    return count if count % 2 == 0 and 4 <= count <= 8 else 0


def ring_order(count):
    return list(range(0, count, 2)) + list(range(count - 1, 0, -2))


def ring_sources(offsets):
    count = lax.axis_size("dp")
    place = lax.axis_index("dp")
    spot = jnp.where(place % 2 == 0, place // 2, count - 1 - place // 2)
    spot = (spot + jnp.asarray(offsets, jnp.int32) + count) % count
    return jnp.where(spot < count // 2, 2 * spot, 2 * (count - 1 - spot) + 1)


def ring_source(offset):
    count = lax.axis_size("dp")
    place = lax.axis_index("dp")
    spot = jnp.where(place % 2 == 0, place // 2, count - 1 - place // 2)
    spot = (spot + offset + count) % count
    return jnp.where(spot < count // 2, 2 * spot, 2 * (count - 1 - spot) + 1)


def ring_move(values, step):
    count = lax.axis_size("dp")
    order = ring_order(count)
    return lax.ppermute(
        values, "dp", [(order[i], order[(i + step) % count]) for i in range(count)]
    )


def half_of(rows):
    return rows // 32 * 16 or rows // 2


class GatherRing:
    def __init__(self, shard, long=1, leads=False):
        count = ring_length()
        self.rows = shard.shape[0]
        self.steps = count // 2
        self.pieces = [shard]
        self.spots = [0]
        self.flying = {}
        self.sent = ()
        if not count:
            self.pieces = [lax.all_gather(shard, "dp", axis=0, tiled=True)]
            return
        self.long = long
        self.leads = leads
        self.taken = 0
        self.flying = {1: shard, -1: shard}

    def step(self, *others):
        if not self.steps:
            return others
        self.flying, others = lax.optimization_barrier((self.flying, others))
        self.taken += 1
        ways = [self.long]
        if (self.taken > 1) if self.leads else (self.taken < self.steps):
            ways.append(-self.long)
        self.sent = tuple(self.flying[way] for way in ways)
        for way in ways:
            self.flying[way] = ring_move(self.flying[way], way)
            self.pieces.append(self.flying[way])
            lag = self.leads and way != self.long
            self.spots.append(-way * (self.taken - int(lag)))
        return others

    def arrived(self):
        return self.flying

    @property
    def offsets(self):
        if not self.steps:
            return jnp.zeros((1,), jnp.int32)
        return ring_sources(self.spots) * self.rows


class ScatterRing:
    def __init__(self, terms, halved=False):
        self.count = ring_length()
        self.halved = halved
        self.terms = terms
        self.flying = {}
        if not self.count:
            size = lax.axis_size("dp")
            parts = [term.reshape(size, -1, term.shape[1]) for term in terms]
            whole = self.joined(parts)
            self.sums = lax.psum_scatter(
                whole.reshape(-1, whole.shape[-1]).astype(BF), "dp", scatter_dimension=0, tiled=True
            ).astype(F32)
            self.steps = 0
            self.sent = ()
            return
        self.steps = self.count // 2
        self.taken = 0
        self.sent = ()

    def joined(self, parts):
        return parts[0] if len(parts) == 1 else jnp.concatenate(parts, axis=-2)

    def term(self, offset):
        parts = []
        for term in self.terms:
            rows = term.shape[0] // self.count
            parts.append(lax.dynamic_slice_in_dim(term, ring_source(offset) * rows, rows, 0))
        return self.joined(parts).astype(F32)

    def step(self, *others):
        if not self.steps:
            return others
        self.taken += 1
        left = self.steps + 1 - self.taken
        if self.taken == 1:
            self.terms, others = lax.optimization_barrier((self.terms, others))
            far = self.term(self.steps)
            half = half_of(far.shape[0])
            values = {1: far[:half], -1: far[half:]} if self.halved else {1: far}
        else:
            self.flying, others = lax.optimization_barrier((self.flying, others))
            values = {way: self.term(way * left) for way in (1, -1)}
            if self.taken == 2 and self.halved:
                up, down = (self.flying[1].astype(F32), self.flying[-1].astype(F32))
                half = up.shape[0]
                values = {
                    1: jnp.concatenate([values[1][:half] + up, values[1][half:]]),
                    -1: jnp.concatenate([values[-1][:half], values[-1][half:] + down]),
                }
            else:
                for way, arrived in self.flying.items():
                    values[way] = values[way] + arrived.astype(F32)
        sent = {way: value.astype(BF) for way, value in values.items()}
        self.sent = tuple(sent.values())
        self.flying = {way: ring_move(value, way) for way, value in sent.items()}
        return others

    def arrived(self):
        return self.flying

    def take(self, arrived):
        self.flying = arrived

    def result(self):
        if not self.steps:
            return self.sums
        return self.term(0) + self.flying[1].astype(F32) + self.flying[-1].astype(F32)


def local(
    tokens,
    segments,
    valid_mask,
    attention_gain,
    query_weight,
    key_weight,
    value_weight,
    query_gain,
    key_gain,
    output_weight,
    feedforward_gain,
    gate_weight,
    up_weight,
    down_weight,
    cotangent,
):
    seq_count = lax.axis_size("seq")
    dp_count = lax.axis_size("dp")
    place = lax.axis_index("seq")
    local_rows = tokens.shape[1]
    row_length = segments.shape[1]
    head_dim = query_gain.shape[0]
    width = tokens.shape[2]
    hidden_width = gate_weight.shape[1]
    query_width = query_weight.shape[1]
    key_width = key_weight.shape[1]
    query_here = query_width // seq_count
    key_here = key_width // seq_count
    hidden_here = hidden_width // seq_count
    weight_rows = query_weight.shape[0]
    own_rows = weight_rows // seq_count
    segment_row = segments[0]
    valid_row = valid_mask[0]

    def low(weight):
        return weight.astype(BF).astype(F32)

    place_array = place.astype(jnp.int32).reshape(1)
    gain_one = attention_gain[:, None]
    gain_two = feedforward_gain[:, None]
    qkv_width = query_here + 2 * key_here
    piece = hidden_width // (dp_count * seq_count)
    kernels_fit = weight_rows % 32 == 0 and own_rows % 8 == 0 and dp_count <= 8

    pack_width = qkv_width + width // seq_count
    (attention_pack,) = call(
        attention_pack_kernel,
        [((weight_rows, pack_width), BF)],
        1,
        (place_array, gain_one),
        58,
        pieces=(query_weight, key_weight, value_weight, output_weight),
        scratch=[pltpu.VMEM((weight_rows, pack_width), F32), pltpu.SemaphoreType.DMA((4,))],
        moved=8 * weight_rows * width,
    )
    if kernels_fit:
        (gate_up_pack,) = call(
            functools.partial(hidden_pack_kernel, dp_count),
            [((weight_rows, 2 * hidden_here), BF)],
            1,
            (place_array, after(gain_two, attention_pack)),
            58,
            pieces=(gate_weight, up_weight),
            scratch=[
                pltpu.VMEM((2, weight_rows, hidden_width), F32),
                pltpu.SemaphoreType.DMA((2, weight_rows // 32)),
            ],
            moved=8 * weight_rows * hidden_width,
        )
    else:

        def hidden_columns(weight):
            split = weight.reshape(weight_rows, dp_count, seq_count, piece)
            mine = lax.dynamic_index_in_dim(split, place, 2, keepdims=False)
            return (low(mine.reshape(weight_rows, hidden_here)) * low(gain_two)).astype(BF)

        gate_up_pack = jnp.concatenate(
            [hidden_columns(gate_weight), hidden_columns(up_weight)], axis=1
        )
    down_pack = lax.dynamic_slice_in_dim(down_weight, place * piece, piece, 0).astype(BF)
    down_pack = after(down_pack, attention_pack)

    order = place ^ jnp.arange(4, dtype=jnp.int32)
    plain = jnp.arange(4, dtype=jnp.int32)

    token_far = swap(tokens[0], 2)
    token_near = swap(tokens[0], 1)
    attention_ring = GatherRing(attention_pack)
    attention_ring.step()
    positions = doc_positions(segment_row)
    starts = jnp.arange(row_length, dtype=jnp.int32) - positions
    cos_wide, sin_wide = rope_tables(positions, head_dim)
    repeats = PAIR // head_dim
    head_gains = jnp.tile(jnp.stack([query_gain, key_gain]), (1, repeats))
    row_starts = starts[:, None]
    usable = valid_row[None, :]
    starts, row_starts, head_gains = attention_ring.step(starts, row_starts, head_gains)
    block_lows = starts[::BLOCK]
    token_far, cos_wide, sin_wide = attention_ring.step(token_far, cos_wide, sin_wide)
    token_pieces = (tokens[0], token_near, token_far, swap(token_far, 1))
    grad_far = swap(after(cotangent[0], token_far), 2)
    grad_near = swap(after(cotangent[0], token_far), 1)
    (gate_up_pack,) = attention_ring.step(gate_up_pack)

    gate_up_ring = GatherRing(after(gate_up_pack, attention_ring.arrived()))
    (grad_far,) = gate_up_ring.step(grad_far)
    grad_row_pieces = (cotangent[0], grad_near, grad_far, swap(grad_far, 1))
    (output_columns,) = pl.pallas_call(
        functools.partial(columns_kernel, qkv_width),
        out_shape=[jax.ShapeDtypeStruct((query_width, width // seq_count), BF)],
        in_specs=scalars(1) + [pl.BlockSpec(memory_space=pltpu.HBM)] * len(attention_ring.pieces),
        out_specs=whole_vmem(1),
        scratch_shapes=[pltpu.SemaphoreType.DMA((1, len(attention_ring.pieces)))],
        compiler_params=pltpu.CompilerParams(vmem_limit_bytes=58 * MEGA),
        cost_estimate=cost(columns_kernel, 0),
    )(attention_ring.offsets, *attention_ring.pieces)
    output_far = swap(output_columns, 2)
    output_near = swap(output_columns, 1)
    projected = call(
        functools.partial(project_kernel, head_dim),
        [
            ((row_length, width), BF),
            ((row_length, query_here + key_here), F32),
            ((row_length, query_here), BF),
            ((row_length, 2 * key_here), BF),
            ((row_length, 2 * key_here), BF),
            ((width, qkv_width), BF),
        ],
        2,
        (place_array, attention_ring.offsets, *token_pieces, cos_wide, sin_wide, head_gains),
        58,
        pieces=attention_ring.pieces,
        scratch=[pltpu.SemaphoreType.DMA((1, len(attention_ring.pieces)))],
        flops=2 * row_length * width * qkv_width,
        moved=12 * row_length * width,
    )
    projected, output_far = gate_up_ring.step(projected, output_far)
    output_pieces = (output_columns, output_near, output_far, swap(output_far, 1))
    unit_one, raw, queries, keys_two, values_two, qkv_weight = projected
    (mixed_here,) = call(
        functools.partial(attend_kernel, head_dim),
        [((row_length, query_here), BF)],
        1,
        (block_lows, queries, keys_two, values_two, row_starts, usable),
        58,
        flops=row_length * width * qkv_width,
        moved=4 * row_length * width,
    )
    mixed_far = swap(mixed_here, 2)
    mixed_near = swap(mixed_here, 1)
    gate_up_ring.step(mixed_here)
    (mixed_far,) = gate_up_ring.step(mixed_far)
    down_ring = GatherRing(after(down_pack, mixed_far), -1, True)
    down_ring.step()
    mixed_pieces = (mixed_here, mixed_near, mixed_far, swap(mixed_far, 1))
    unit_two, after_here = call(
        middle_kernel,
        [((row_length, width), BF), ((local_rows, width), F32)],
        1,
        (place_array, *token_pieces, *mixed_pieces, *output_pieces),
        18,
        scratch=[pltpu.VMEM((local_rows, width), F32)],
        flops=2 * row_length * width * width,
        moved=10 * row_length * width,
    )
    (unit_two,) = down_ring.step(unit_two)

    rows_each = row_length // 4
    hidden, gate_factor, up_factor = block_call(
        hidden_kernel,
        [((row_length, hidden_here), BF, (rows_each, hidden_here), row_block)] * 3,
        (gate_up_ring.offsets,),
        [(unit_two, (rows_each, width), row_block)],
        28,
        gate_up_ring.pieces,
        [
            pltpu.VMEM((width, 2 * hidden_here), BF),
            pltpu.SemaphoreType.DMA((1, len(gate_up_ring.pieces))),
        ],
        4 * row_length * width * hidden_here,
        8 * row_length * hidden_here + 4 * width * hidden_here,
    )
    hidden, gate_factor, up_factor = down_ring.step(hidden, gate_factor, up_factor)
    grad_rows = jnp.concatenate(grad_row_pieces)
    down_scatter = ScatterRing([mm_tn(hidden, grad_rows)])
    (down_scatter.terms,) = down_ring.step(down_scatter.terms)
    down_scatter.step()
    gate_up_grad, down_all = block_call(
        hidden_grad_kernel,
        [
            ((row_length, 2 * hidden_here), BF, (rows_each, 2 * hidden_here), row_block),
            ((hidden_here, width), BF, (hidden_here, width), first_block),
        ],
        (down_ring.offsets,),
        [
            (grad_rows, (rows_each, width), row_block),
            (gate_factor, (rows_each, hidden_here), row_block),
            (up_factor, (rows_each, hidden_here), row_block),
        ],
        24,
        down_ring.pieces,
        [pltpu.SemaphoreType.DMA((1, len(down_ring.pieces)))],
        2 * row_length * width * hidden_here,
        8 * row_length * hidden_here + 4 * width * hidden_here,
    )

    (gate_up_grad,) = down_scatter.step(gate_up_grad)
    keep, send = split_product(
        gate_up_grad, (width, 2 * hidden_here), gate_up_ring.offsets, gate_up_ring.pieces, True, plain
    )
    keep, send = down_scatter.step(keep, send)

    def halves(keep, near):
        return (
            keep[:local_rows] + near[:local_rows].astype(F32),
            (keep[local_rows:] + near[local_rows:].astype(F32)).astype(BF),
        )

    half_sum, half_send = halves(keep, swap(send, 1))
    half_send, unit_two = lax.optimization_barrier((half_send, unit_two))
    arrived = swap(half_send, 2)
    gate_up_scatter = ScatterRing([mm_tn(unit_two, gate_up_grad).astype(BF)], True)
    gate_up_scatter.step()
    unit_here, factor_here = rms_stats(after_here)
    grad_after = cotangent[0].astype(F32) + rms_back(
        half_sum + arrived.astype(F32), unit_here, factor_here
    )
    branch = grad_after.astype(BF)
    branch_far = swap(branch, 2)
    branch_near = swap(branch, 1)
    gate_up_scatter.step(branch)
    keep, send = split_product(
        after(hidden, branch, gate_up_scatter.sent),
        (hidden_here, width),
        jnp.zeros((1,), jnp.int32),
        [down_all],
        False,
        plain,
    )
    keep, send, branch_far = gate_up_scatter.step(keep, send, branch_far)
    down_scatter.step(branch_far)
    branch_pieces = (branch, branch_near, branch_far, swap(branch_far, 1))
    half_sum, half_send = halves(keep, swap(send, 1))
    chunk_rows = query_width // (dp_count * seq_count)
    grad_mixed, output_terms = call(
        functools.partial(output_grad_kernel, chunk_rows),
        [
            ((row_length, query_here), BF),
            ((query_here * width // qkv_width, qkv_width), F32),
        ],
        1,
        (place_array, *branch_pieces, mixed_here, *output_pieces),
        14,
        scratch=[pltpu.VMEM((query_here, width), F32)],
        flops=4 * row_length * width * query_here,
        moved=8 * row_length * width,
    )

    grad_mixed, half_send = gate_up_scatter.step(grad_mixed, half_send)
    arrived = swap(half_send, 2)
    qkv_grad, gain_terms = call(
        functools.partial(back_kernel, head_dim),
        [((row_length, qkv_width), BF), ((8, PAIR), F32)],
        1,
        (block_lows, after(grad_mixed, gate_up_scatter.sent), queries, keys_two, values_two, raw)
        + (cos_wide, sin_wide, head_gains, row_starts, usable),
        24,
        scratch=[pltpu.VMEM((row_length, 2 * key_here), F32)] * 2,
        flops=4 * row_length * width * qkv_width,
        moved=12 * row_length * width,
    )
    qkv_grad, gain_terms, arrived, gate_up_arrived, down_arrived = lax.optimization_barrier(
        (qkv_grad, gain_terms, arrived, gate_up_scatter.arrived(), down_scatter.arrived())
    )
    down_scatter.take(down_arrived)
    gate_up_scatter.take(gate_up_arrived)
    layer_out = (after_here + half_sum + arrived.astype(F32)).astype(BF)
    gain_rows = jnp.concatenate([gain_terms[0:1], gain_terms[1:2]], axis=1)
    gain_rows = jnp.pad(gain_rows, ((0, 15), (0, qkv_width - 2 * PAIR)))
    packed = jnp.concatenate(
        [
            mm_tn(unit_one, qkv_grad).reshape(dp_count, weight_rows, qkv_width),
            output_terms.reshape(dp_count, -1, qkv_width),
            jnp.broadcast_to(gain_rows, (dp_count, *gain_rows.shape)),
        ],
        axis=1,
    )
    attention_scatter = ScatterRing([packed.reshape(-1, qkv_width)])
    attention_scatter.step()
    gate_up_scatter.take(after(gate_up_scatter.arrived(), attention_scatter.sent))
    gate_up_sums = gate_up_scatter.result().astype(BF)
    keep, send = split_product(
        after(qkv_grad, gate_up_sums),
        (width, qkv_width),
        jnp.zeros((1,), jnp.int32),
        [qkv_weight],
        True,
        order,
    )
    keep, send = attention_scatter.step(keep, send)
    gate_up_sums = after(gate_up_sums, attention_scatter.sent)
    hidden_own = lax.all_to_all(
        gate_up_sums.reshape(seq_count, own_rows, -1), "seq", split_axis=0, concat_axis=0, tiled=True
    )
    half_sum, half_send = halves(keep, swap(send, 1))
    (half_send,) = attention_scatter.step(half_send)
    arrived = swap(half_send, 2)
    for _ in range(attention_scatter.steps - 3):
        (arrived,) = attention_scatter.step(arrived)
        hidden_own = after(hidden_own, attention_scatter.sent)
    unit_tokens, factor_tokens = rms_stats(tokens[0].astype(F32))
    token_grad = (
        grad_after + rms_back(half_sum + arrived.astype(F32), unit_tokens, factor_tokens)
    ).astype(BF)

    down_sums = down_scatter.result()
    attention_sums = attention_scatter.result().astype(BF)
    qkv_sums = attention_sums[:weight_rows]
    output_sums = jnp.concatenate(
        [
            attention_sums[weight_rows + part * chunk_rows : weight_rows + (part + 1) * chunk_rows]
            for part in range(width // qkv_width)
        ],
        axis=1,
    )

    def own(weight):
        return lax.dynamic_slice_in_dim(weight, place * own_rows, own_rows, 0)

    gain_row = attention_sums[-16:]
    qkv_pieces = []
    for bits in range(4):
        part = lax.dynamic_slice_in_dim(qkv_sums, (place ^ bits) * own_rows, own_rows, 0)
        part = after(jnp.concatenate([part, gain_row]), arrived)
        qkv_pieces.append(swap(part, bits) if bits else part)
    gain_sums = sum(piece[own_rows : own_rows + 1].astype(F32) for piece in qkv_pieces)
    gain_sums = jnp.sum(gain_sums[0, : 2 * PAIR].reshape(2, repeats, head_dim), axis=1)
    if kernels_fit:
        gate_grad, up_grad, feed_gain_grad = placed_call(
            functools.partial(hidden_owner_kernel, dp_count),
            [((own_rows, hidden_width), F32)] * 2 + [((1, own_rows), F32)],
            place_array,
            (hidden_own, gate_weight, up_weight, gain_two),
            [
                (hidden_own.shape, lambda i, place: (0, 0, 0)),
                ((own_rows, hidden_width), own_rows_block),
                ((own_rows, hidden_width), own_rows_block),
                ((own_rows, 1), own_rows_block),
            ],
            58,
            moved=20 * own_rows * hidden_width,
        )
        query_grad, key_grad, value_grad, attention_gain_grad = placed_call(
            attention_owner_kernel,
            [((own_rows, query_width), F32)]
            + [((own_rows, key_width), F32)] * 2
            + [((1, own_rows), F32)],
            place_array,
            (*qkv_pieces, query_weight, key_weight, value_weight, gain_one),
            [((own_rows + 16, qkv_width), everything)] * 4
            + [
                ((own_rows, query_width), own_rows_block),
                ((own_rows, key_width), own_rows_block),
                ((own_rows, key_width), own_rows_block),
                ((own_rows, 1), own_rows_block),
            ],
            58,
            moved=20 * own_rows * query_width,
        )
    else:
        spread = jnp.stack(qkv_pieces)[order, :own_rows].astype(F32)

        def joined(first, size):
            return jnp.swapaxes(spread[:, :, first : first + size], 0, 1).reshape(own_rows, -1)

        query_own = joined(0, query_here)
        key_own = joined(query_here, key_here)
        value_own = joined(query_here + key_here, key_here)
        attention_gain_grad = (
            jnp.sum(own(low(query_weight)) * query_own, axis=1)
            + jnp.sum(own(low(key_weight)) * key_own, axis=1)
            + jnp.sum(own(low(value_weight)) * value_own, axis=1)
        )
        gain_own = own(low(gain_one))
        query_grad, key_grad, value_grad = (
            query_own * gain_own,
            key_own * gain_own,
            value_own * gain_own,
        )
        hidden_own = hidden_own.reshape(seq_count, own_rows, 2, dp_count, piece)
        hidden_own = jnp.transpose(hidden_own, (2, 1, 3, 0, 4))
        hidden_own = hidden_own.reshape(2, own_rows, hidden_width).astype(F32)
        feed_gain_grad = jnp.sum(own(low(gate_weight)) * hidden_own[0], axis=1) + jnp.sum(
            own(low(up_weight)) * hidden_own[1], axis=1
        )
        gain_own = own(low(gain_two))
        gate_grad, up_grad = (hidden_own[0] * gain_own, hidden_own[1] * gain_own)

    moves = [
        (dp * seq_count + seq, seq * dp_count + dp)
        for dp in range(dp_count)
        for seq in range(seq_count)
    ]
    output_own = lax.ppermute(output_sums, ("dp", "seq"), moves).astype(F32)

    return (
        layer_out.reshape(1, local_rows, -1),
        token_grad.reshape(1, local_rows, -1),
        attention_gain_grad.reshape(own_rows),
        query_grad,
        key_grad,
        value_grad,
        gain_sums[0],
        gain_sums[1],
        output_own,
        feed_gain_grad.reshape(own_rows),
        gate_grad,
        up_grad,
        down_sums,
    )


def solution(mesh):
    in_specs = (
        P("dp", "seq", None),
        P("dp", None),
        P("dp", None),
        P("dp"),
        P("dp", None),
        P("dp", None),
        P("dp", None),
        P(),
        P(),
        P("dp", None),
        P("dp"),
        P("dp", None),
        P("dp", None),
        P("dp", None),
        P("dp", "seq", None),
    )
    out_specs = (
        P("dp", "seq", None),
        P("dp", "seq", None),
        P(("dp", "seq")),
        P(("dp", "seq"), None),
        P(("dp", "seq"), None),
        P(("dp", "seq"), None),
        P(),
        P(),
        P(("dp", "seq"), None),
        P(("dp", "seq")),
        P(("dp", "seq"), None),
        P(("dp", "seq"), None),
        P(("dp", "seq"), None),
    )
    return jax.shard_map(local, mesh=mesh, in_specs=in_specs, out_specs=out_specs, check_vma=False)
```

profile of v0, /device:TPU:0, one launch (start us, length us, event | category | flops | bytes accessed | tf_op | source)
XLA Modules:
  0.0 280.5 jit_solution(11223038367828340557)
XLA Ops:
  4.9 3.0 %collective-permute-start.1 = (bf16[128,768]{1,0:T(8,128)(2,1)}, bf16[128,768]{1,0:T(8,128)(2,1)}, u32[]{:S(2)}, u32[]{:S(2)}) collective-permute-start(bf16[128,768]{1,0:T(8,128)(2,1)} %shard_map.291.rest_0_), channel_id=1, source_target_pairs={{0,4},{8,0},{16,8},{24,16},{28,24},{20,28},{12,20},{4,12},{1,5},{9... | collective-permute-start | bytes 589832 | tf_op jit(solution)/shard_map/ppermute | solution.py:785
  16.6 3.0 %fusion.8 = (f32[1024,128]{1,0:T(8,128)}, f32[1024,128]{1,0:T(8,128)}) fusion(f32[128]{0:T(128)S(1)} %get-tuple-element.307, f32[128]{0:T(128)S(1)} %get-tuple-element.308, f32[1024]{0:T(1024)S(1)} %get-tuple-element.267), kind=kLoop, calls=%fused_computation.42 | loop fusion | flops 262144 | bytes 1053696 | tf_op jit(solution)/shard_map/mul | solution.py:63
  26.8 4.2 %shard_map.292.rest_0_ = bf16[128,2304]{1,0:T(8,128)(2,1)} custom-call(s32[1]{0:T(128)} %bitcast.place_ref, f32[128,1]{1,0:T(8,128)} %copy.39.gain_ref, f32[128,4608]{1,0:T(8,128)} %gate_ref.3, f32[128,4608]{1,0:T(8,128)} %up_ref.3), custom_call_target="tpu_custom_call" | custom-call | flops 2415000064 | tf_op jit(solution)/shard_map/pallas_call | solution.py:677
  33.9 4.8 %collective-permute-done.9.rest_7_ = bf16[128,768]{1,0:T(8,128)(2,1)S(1)} collective-permute-done((bf16[128,768]{1,0:T(8,128)(2,1)S(1)}, bf16[128,768]{1,0:T(8,128)(2,1)S(1)}, u32[]{:S(2)}, u32[]{:S(2)}) %collective-permute-start.9) | collective-permute-done | bytes 196640 | tf_op jit(solution)/shard_map/ppermute | solution.py:785
  40.7 2.7 shard_map.294.w0_ref
  44.8 9.0 %shard_map.293 = (bf16[1024,1024]{1,0:T(8,128)(2,1)}, f32[1024,384]{1,0:T(8,128)}, bf16[1024,256]{1,0:T(8,128)(2,1)}, bf16[1024,256]{1,0:T(8,128)(2,1)}, bf16[10...) custom-call(s32[1]{0:T(128)} %bitcast.place_ref, s32[8]{0:T(128)} %fusion.20.offset_ref, bf16[256,1024]{1,0:T(8,128)(2,1)} %bitcast.42, ...), custom_call_target="tpu_custom_call" | custom-call | flops 5462499840 | tf_op jit(solution)/shard_map/pallas_call | solution.py:677
  57.7 7.2 %shard_map.295.o0_ref.mixed_ref = bf16[1024,256]{1,0:T(8,128)(2,1)} custom-call(s32[8]{0:T(128)} %slice.125.low_ref, bf16[1024,256]{1,0:T(8,128)(2,1)} %get-tuple-element.163.query_ref, bf16[1024,256]{1,0:T(8,128)(2,1)} %get-tuple-element.164.key_ref, bf16[1024,256]{1,0:T(8,128)(2,1)} %get-tuple-element.165.value_ref, ...), custom_call_target="tpu_custom_call" | custom-call | flops 4024999936 | tf_op jit(solution)/shard_map/pallas_call | solution.py:677
  72.4 8.4 %collective-permute-done.19.o2_ref = bf16[1024,256]{1,0:T(8,128)(2,1)} collective-permute-done((bf16[1024,256]{1,0:T(8,128)(2,1)}, bf16[1024,256]{1,0:T(8,128)(2,1)}, u32[]{:S(2)}, u32[]{:S(2)}) %collective-permute-start.19) | collective-permute-done | bytes 524320 | tf_op jit(solution)/shard_map/ppermute | solution.py:744
  87.2 6.5 %shard_map.296 = (bf16[1024,1024]{1,0:T(8,128)(2,1)S(1)}, f32[256,1024]{1,0:T(8,128)S(1)}) custom-call(s32[1]{0:T(128)} %bitcast.place_ref, bf16[256,1024]{1,0:T(8,128)(2,1)S(1)} %bitcast.45, bf16[256,1024]{1,0:T(8,128)(2,1)} %collective-permute-done.x1_ref, bf16[256,1024]{1,0:T(8,128)(2,1)} %collective-permute-done.5.x2_ref, ...), custom_call_target="tpu_custom_call" | custom-call | flops 2875000064 | tf_op jit(solution)/shard_map/pallas_call | solution.py:677
  98.2 8.9 %shard_map.297 = (bf16[1024,1152]{1,0:T(8,128)(2,1)S(1)}, bf16[1024,1152]{1,0:T(8,128)(2,1)S(1)}, bf16[1024,1152]{1,0:T(8,128)(2,1)S(1)}) custom-call(s32[8]{0:T(128)S(1)} %copy-done.22, bf16[1024,1024]{1,0:T(8,128)(2,1)S(1)} %get-tuple-element.202.unit_ref, bf16[128,2304]{1,0:T(8,128)(2,1)S(1)} %copy-done.12, ...), custom_call_target="tpu_custom_call" | custom-call | flops 5175000064 | tf_op jit(solution)/shard_map/pallas_call | solution.py:691
  109.3 3.7 %fusion.24 = f32[1152,1024]{1,0:T(8,128)S(1)} fusion(bf16[1024,1152]{1,0:T(8,128)(2,1)S(1)} %get-tuple-element.206.left_ref, bf16[256,1024]{1,0:T(8,128)(2,1)S(1)} %collective-permute-done.30, bf16[256,1024]{1,0:T(8,128)(2,1)} %collective-permute-done.10, bf16[256,1024]{1,0:T(8,128)(2,1)S(1)} %collective-permute-done.29, bf16[256,1024]{1,0:T(8,128)(2,1)S(1)} %bitcast.56), kind=kOutput, calls=%fused_computation.113 | convolution fusion | flops 2424307712 | bytes 9175040 | tf_op jit(solution)/shard_map/dot_general | solution.py:23
  121.3 4.5 %collective-permute-done.33.rest_6_ = bf16[144,1024]{1,0:T(8,128)(2,1)S(1)} collective-permute-done((bf16[144,1024]{1,0:T(8,128)(2,1)S(1)}, bf16[144,1024]{1,0:T(8,128)(2,1)S(1)}, u32[]{:S(2)}, u32[]{:S(2)}) %collective-permute-start.33) | collective-permute-done | bytes 294944 | tf_op jit(solution)/shard_map/ppermute | solution.py:785
  126.7 5.0 %shard_map.298 = (bf16[1024,2304]{1,0:T(8,128)(2,1)S(1)}, bf16[1152,1024]{1,0:T(8,128)(2,1)S(1)}) custom-call(s32[8]{0:T(128)S(1)} %fusion.21.offset_ref, bf16[1024,1024]{1,0:T(8,128)(2,1)S(1)} %pad_maximum_fusion.1.grad_ref, bf16[1024,1152]{1,0:T(8,128)(2,1)S(1)} %get-tuple-element.191.gate_factor_ref, ...), custom_call_target="tpu_custom_call" | custom-call | flops 3104999936 | tf_op jit(solution)/shard_map/pallas_call | solution.py:691
  132.9 9.7 %shard_map.299 = (f32[512,1024]{1,0:T(8,128)S(1)}, bf16[512,1024]{1,0:T(8,128)(2,1)}) custom-call(s32[4]{0:T(128)S(1)} %iota.55.order_ref, s32[8]{0:T(128)S(1)} %copy-done.22, bf16[1024,2304]{1,0:T(8,128)(2,1)S(1)} %get-tuple-element.197.left_ref, bf16[128,2304]{1,0:T(8,128)(2,1)S(1)} %copy-done.12, bf16[128,2304]{1,0:T(8,128)(2,1)} %collective-permute-done.12.rest_1_, ...), custom_call_target="tpu_custom_call" | custom-call | flops 5844113920 | tf_op jit(solution)/shard_map/pallas_call | solution.py:691
  142.9 2.8 collective-permute-done.36
  147.6 7.7 %convolution_convert_fusion = bf16[1024,2304]{1,0:T(8,128)(2,1)S(1)} fusion(bf16[1024,1024]{1,0:T(8,128)(2,1)S(1)} %copy-done.28, bf16[1024,2304]{1,0:T(8,128)(2,1)} %copy-done.24), kind=kOutput, calls=%fused_computation | convolution fusion | flops 4834197504 | bytes 11534336 | tf_op jit(solution)/shard_map/dot_general | solution.py:23
  157.6 3.4 %collective-permute-done.39 = bf16[256,1024]{1,0:T(8,128)(2,1)S(1)} collective-permute-done((bf16[256,1024]{1,0:T(8,128)(2,1)S(1)}, bf16[256,1024]{1,0:T(8,128)(2,1)S(1)}, u32[]{:S(2)}, u32[]{:S(2)}) %collective-permute-start.39) | collective-permute-done | bytes 524320 | tf_op jit(solution)/shard_map/ppermute | solution.py:744
  173.9 4.3 %shard_map.300 = (f32[512,1024]{1,0:T(8,128)S(1)}, bf16[512,1024]{1,0:T(8,128)(2,1)S(1)}) custom-call(s32[4]{0:T(128)S(1)} %iota.56.order_ref, s32[1]{0:T(128)} %constant.399.clone.1.offset_ref, bf16[1024,1152]{1,0:T(8,128)(2,1)S(1)} %copy-done.31, bf16[1152,1024]{1,0:T(8,128)(2,1)S(1)} %copy-done.26), custom_call_target="tpu_custom_call" | custom-call | flops 3065806848 | tf_op jit(solution)/shard_map/pallas_call | solution.py:691
  192.5 2.8 %shard_map.301 = (bf16[1024,256]{1,0:T(8,128)(2,1)S(1)}, f32[512,512]{1,0:T(8,128)S(1)}) custom-call(s32[1]{0:T(128)} %bitcast.place_ref, bf16[256,1024]{1,0:T(8,128)(2,1)S(1)} %copy-done.7, bf16[256,1024]{1,0:T(8,128)(2,1)S(1)} %collective-permute-done.46.g1_ref, bf16[256,1024]{1,0:T(8,128)(2,1)S(1)} %collective-permute-done.42.g2_ref, ...), custom_call_target="tpu_custom_call" | custom-call | flops 1724999936 | tf_op jit(solution)/shard_map/pallas_call | solution.py:677
  195.7 7.6 %collective-permute-done.44 = bf16[128,2304]{1,0:T(8,128)(2,1)S(1)} collective-permute-done((bf16[128,2304]{1,0:T(8,128)(2,1)S(1)}, bf16[128,2304]{1,0:T(8,128)(2,1)S(1)}, u32[]{:S(2)}, u32[]{:S(2)}) %collective-permute-start.44) | collective-permute-done | bytes 589856 | tf_op jit(solution)/shard_map/ppermute | solution.py:785
  207.3 15.7 %shard_map.302 = (bf16[1024,512]{1,0:T(8,128)(2,1)S(1)}, f32[8,128]{1,0:T(8,128)S(1)}) custom-call(s32[8]{0:T(128)S(1)} %copy-done.23, bf16[1024,256]{1,0:T(8,128)(2,1)S(1)} %get-tuple-element.219.grad_ref, bf16[1024,256]{1,0:T(8,128)(2,1)S(1)} %copy-done.33, bf16[1024,256]{1,0:T(8,128)(2,1)S(1)} %copy-done.34, bf16[1024,256]{1,0:T(8,128)(2,1)S(1)} %copy-done.35, ...), custom_call_target="tpu_custom_call" | custom-call | flops 8970000384 | tf_op jit(solution)/shard_map/pallas_call | solution.py:677
  228.5 3.8 %shard_map.303 = (f32[512,1024]{1,0:T(8,128)S(1)}, bf16[512,1024]{1,0:T(8,128)(2,1)}) custom-call(s32[4]{0:T(128)S(1)} %iota_xor_fusion.order_ref, s32[1]{0:T(128)} %constant.399.clone.1.offset_ref, bf16[1024,512]{1,0:T(8,128)(2,1)S(1)} %get-tuple-element.237.left_ref, bf16[1024,512]{1,0:T(8,128)(2,1)S(1)} %copy-done.29), custom_call_target="tpu_custom_call" | custom-call | flops 1522303104 | tf_op jit(solution)/shard_map/pallas_call | solution.py:691
  254.2 4.2 %all-to-all-start = ((bf16[4,32,2304]{2,1,0:T(8,128)(2,1)}), bf16[4,32,2304]{2,1,0:T(8,128)(2,1)}, u32[]{:S(2)}, u32[]{:S(2)}) async-start(bf16[4,32,2304]{2,1,0:T(8,128)(2,1)} %bitcast.52), calls=%async_computation | async-start | bytes 1179648 | tf_op jit(solution)/shard_map/all_to_all | solution.py:1209
  268.0 3.0 %shard_map.305 = (f32[32,4608]{1,0:T(8,128)}, f32[32,4608]{1,0:T(8,128)}, f32[1,32]{1,0:T(1,128)}) custom-call(s32[1]{0:T(128)} %bitcast.place_ref, bf16[4,32,2304]{2,1,0:T(8,128)(2,1)} %all-to-all-done.sums_ref, f32[128,4608]{1,0:T(8,128)} %gate_ref.3, f32[128,4608]{1,0:T(8,128)} %up_ref.3, f32[128,1]{1,0:T(8,128)} %copy.41.gain_ref), custom_call_target="tpu_custom_call" | custom-call | flops 1782499968 | tf_op jit(solution)/shard_map/pallas_call | solution.py:627
  (340 shorter events, 142.8 us)
Async XLA Ops:
  8.0 14.0 %collective-permute-start.5 = (bf16[256,1024]{1,0:T(8,128)(2,1)S(1)}, bf16[256,1024]{1,0:T(8,128)(2,1)}, u32[]{:S(2)}, u32[]{:S(2)}) collective-permute-start(bf16[256,1024]{1,0:T(8,128)(2,1)S(1)} %bitcast.43), channel_id=1, source_target_pairs={{0,2},{1,3},{2,0},{3,1},{4,6},{5,7},{6,4},{7,5},{8,10},{9,11},{10,... | collective-permute-start | bytes 1572872 | tf_op jit(solution)/shard_map/ppermute | solution.py:744
  22.1 16.6 %collective-permute-start.10 = (bf16[256,1024]{1,0:T(8,128)(2,1)}, bf16[256,1024]{1,0:T(8,128)(2,1)}, u32[]{:S(2)}, u32[]{:S(2)}) collective-permute-start(bf16[256,1024]{1,0:T(8,128)(2,1)} %bitcast.54), channel_id=1, source_target_pairs={{0,2},{1,3},{2,0},{3,1},{4,6},{5,7},{6,4},{7,5},{8,10},{9,11},{10,... | collective-permute-start | bytes 1572872 | tf_op jit(solution)/shard_map/ppermute | solution.py:744
  23.5 20.4 %collective-permute-start = (bf16[256,1024]{1,0:T(8,128)(2,1)S(1)}, bf16[256,1024]{1,0:T(8,128)(2,1)}, u32[]{:S(2)}, u32[]{:S(2)}) collective-permute-start(bf16[256,1024]{1,0:T(8,128)(2,1)S(1)} %bitcast.44), channel_id=1, source_target_pairs={{0,1},{1,0},{2,3},{3,2},{4,5},{5,4},{6,7},{7,6},{8,9},{9,8},{10,11... | collective-permute-start | bytes 1572872 | tf_op jit(solution)/shard_map/ppermute | solution.py:744
  24.3 19.7 %collective-permute-start.6 = (bf16[256,1024]{1,0:T(8,128)(2,1)}, bf16[256,1024]{1,0:T(8,128)(2,1)S(1)}, u32[]{:S(2)}, u32[]{:S(2)}) collective-permute-start(bf16[256,1024]{1,0:T(8,128)(2,1)} %collective-permute-done.5.x2_ref), channel_id=1, source_target_pairs={{0,1},{1,0},{2,3},{3,2},{4,5},{5,4},{6,7},{7,6},{8,9},{9,8},{10,11... | collective-permute-start | bytes 1572872 | tf_op jit(solution)/shard_map/ppermute | solution.py:744
  38.7 16.4 %collective-permute-start.11 = (bf16[128,2304]{1,0:T(8,128)(2,1)}, bf16[128,2304]{1,0:T(8,128)(2,1)S(1)}, u32[]{:S(2)}, u32[]{:S(2)}) collective-permute-start(bf16[128,2304]{1,0:T(8,128)(2,1)} %shard_map.292.rest_0_), channel_id=1, source_target_pairs={{0,4},{8,0},{16,8},{24,16},{28,24},{20,28},{12,20},{4,12},{1,5},{9... | collective-permute-start | bytes 1769480 | tf_op jit(solution)/shard_map/ppermute | solution.py:785
  40.2 14.8 %collective-permute-start.12 = (bf16[128,2304]{1,0:T(8,128)(2,1)}, bf16[128,2304]{1,0:T(8,128)(2,1)}, u32[]{:S(2)}, u32[]{:S(2)}) collective-permute-start(bf16[128,2304]{1,0:T(8,128)(2,1)} %shard_map.292.rest_0_), channel_id=1, source_target_pairs={{0,8},{8,16},{16,24},{24,28},{28,20},{20,12},{12,4},{4,0},{1,9},{9... | collective-permute-start | bytes 1769480 | tf_op jit(solution)/shard_map/ppermute | solution.py:785
  82.2 16.0 %collective-permute-start.26 = (bf16[128,2304]{1,0:T(8,128)(2,1)}, bf16[128,2304]{1,0:T(8,128)(2,1)}, u32[]{:S(2)}, u32[]{:S(2)}) collective-permute-start(bf16[128,2304]{1,0:T(8,128)(2,1)} %collective-permute-done.18.rest_5_), channel_id=1, source_target_pairs={{0,8},{8,16},{16,24},{24,28},{28,20},{20,12},{12,4},{4,0},{1,9},{9... | collective-permute-start | bytes 1769480 | tf_op jit(solution)/shard_map/ppermute | solution.py:785
  84.5 24.8 %collective-permute-start.29 = (bf16[256,1024]{1,0:T(8,128)(2,1)}, bf16[256,1024]{1,0:T(8,128)(2,1)S(1)}, u32[]{:S(2)}, u32[]{:S(2)}) collective-permute-start(bf16[256,1024]{1,0:T(8,128)(2,1)} %bitcast.55), channel_id=1, source_target_pairs={{0,1},{1,0},{2,3},{3,2},{4,5},{5,4},{6,7},{7,6},{8,9},{9,8},{10,11... | collective-permute-start | bytes 1572872 | tf_op jit(solution)/shard_map/ppermute | solution.py:744
  84.6 24.7 %collective-permute-start.30 = (bf16[256,1024]{1,0:T(8,128)(2,1)}, bf16[256,1024]{1,0:T(8,128)(2,1)S(1)}, u32[]{:S(2)}, u32[]{:S(2)}) collective-permute-start(bf16[256,1024]{1,0:T(8,128)(2,1)} %collective-permute-done.10), channel_id=1, source_target_pairs={{0,1},{1,0},{2,3},{3,2},{4,5},{5,4},{6,7},{7,6},{8,9},{9,8},{10,11... | collective-permute-start | bytes 1572872 | tf_op jit(solution)/shard_map/ppermute | solution.py:744
  117.9 13.8 %collective-permute-start.32 = (bf16[144,1024]{1,0:T(8,128)(2,1)S(1)}, bf16[144,1024]{1,0:T(8,128)(2,1)S(1)}, u32[]{:S(2)}, u32[]{:S(2)}) collective-permute-start(bf16[144,1024]{1,0:T(8,128)(2,1)S(1)} %get-tuple-element.283), channel_id=1, source_target_pairs={{0,8},{8,16},{16,24},{24,28},{28,20},{20,12},{12,4},{4,0},{1,9},{9... | collective-permute-start | bytes 884744 | tf_op jit(solution)/shard_map/ppermute | solution.py:785
  120.0 22.7 %collective-permute-start.31 = (bf16[144,1024]{1,0:T(8,128)(2,1)S(1)}, bf16[144,1024]{1,0:T(8,128)(2,1)S(1)}, u32[]{:S(2)}, u32[]{:S(2)}) collective-permute-start(bf16[144,1024]{1,0:T(8,128)(2,1)S(1)} %get-tuple-element.284), channel_id=1, source_target_pairs={{0,4},{8,0},{16,8},{24,16},{28,24},{20,28},{12,20},{4,12},{1,5},{9... | collective-permute-start | bytes 884744 | tf_op jit(solution)/shard_map/ppermute | solution.py:785
  146.9 14.0 %collective-permute-start.39 = (bf16[256,1024]{1,0:T(8,128)(2,1)S(1)}, bf16[256,1024]{1,0:T(8,128)(2,1)S(1)}, u32[]{:S(2)}, u32[]{:S(2)}) collective-permute-start(bf16[256,1024]{1,0:T(8,128)(2,1)S(1)} %add_convert_fusion.8), channel_id=1, source_target_pairs={{0,2},{1,3},{2,0},{3,1},{4,6},{5,7},{6,4},{7,5},{8,10},{9,11},{10,... | collective-permute-start | bytes 1572872 | tf_op jit(solution)/shard_map/ppermute | solution.py:744
  165.1 16.4 %collective-permute-start.41 = (bf16[128,2304]{1,0:T(8,128)(2,1)S(1)}, bf16[128,2304]{1,0:T(8,128)(2,1)}, u32[]{:S(2)}, u32[]{:S(2)}) collective-permute-start(bf16[128,2304]{1,0:T(8,128)(2,1)S(1)} %pad_maximum_fusion.3), channel_id=1, source_target_pairs={{0,8},{8,16},{16,24},{24,28},{28,20},{20,12},{12,4},{4,0},{1,9},{9... | collective-permute-start | bytes 1769480 | tf_op jit(solution)/shard_map/ppermute | solution.py:785
  166.4 16.4 %collective-permute-start.40 = (bf16[128,2304]{1,0:T(8,128)(2,1)S(1)}, bf16[128,2304]{1,0:T(8,128)(2,1)}, u32[]{:S(2)}, u32[]{:S(2)}) collective-permute-start(bf16[128,2304]{1,0:T(8,128)(2,1)S(1)} %pad_maximum_fusion.2), channel_id=1, source_target_pairs={{0,4},{8,0},{16,8},{24,16},{28,24},{20,28},{12,20},{4,12},{1,5},{9... | collective-permute-start | bytes 1769480 | tf_op jit(solution)/shard_map/ppermute | solution.py:785
  170.2 16.8 %collective-permute-start.51 = (bf16[144,1024]{1,0:T(8,128)(2,1)S(1)}, bf16[144,1024]{1,0:T(8,128)(2,1)S(1)}, u32[]{:S(2)}, u32[]{:S(2)}) collective-permute-start(bf16[144,1024]{1,0:T(8,128)(2,1)S(1)} %get-tuple-element.272), channel_id=1, source_target_pairs={{0,4},{8,0},{16,8},{24,16},{28,24},{20,28},{12,20},{4,12},{1,5},{9... | collective-permute-start | bytes 884744 | tf_op jit(solution)/shard_map/ppermute | solution.py:785
  170.9 16.1 %collective-permute-start.52 = (bf16[144,1024]{1,0:T(8,128)(2,1)S(1)}, bf16[144,1024]{1,0:T(8,128)(2,1)S(1)}, u32[]{:S(2)}, u32[]{:S(2)}) collective-permute-start(bf16[144,1024]{1,0:T(8,128)(2,1)S(1)} %get-tuple-element.271), channel_id=1, source_target_pairs={{0,8},{8,16},{16,24},{24,28},{28,20},{20,12},{12,4},{4,0},{1,9},{9... | collective-permute-start | bytes 884744 | tf_op jit(solution)/shard_map/ppermute | solution.py:785
  187.0 16.3 %collective-permute-start.44 = (bf16[128,2304]{1,0:T(8,128)(2,1)S(1)}, bf16[128,2304]{1,0:T(8,128)(2,1)S(1)}, u32[]{:S(2)}, u32[]{:S(2)}) collective-permute-start(bf16[128,2304]{1,0:T(8,128)(2,1)S(1)} %get-tuple-element.276), channel_id=1, source_target_pairs={{0,4},{8,0},{16,8},{24,16},{28,24},{20,28},{12,20},{4,12},{1,5},{9... | collective-permute-start | bytes 1769480 | tf_op jit(solution)/shard_map/ppermute | solution.py:785
  187.9 16.3 %collective-permute-start.45 = (bf16[128,2304]{1,0:T(8,128)(2,1)S(1)}, bf16[128,2304]{1,0:T(8,128)(2,1)S(1)}, u32[]{:S(2)}, u32[]{:S(2)}) collective-permute-start(bf16[128,2304]{1,0:T(8,128)(2,1)S(1)} %get-tuple-element.275), channel_id=1, source_target_pairs={{0,8},{8,16},{16,24},{24,28},{28,20},{20,12},{12,4},{4,0},{1,9},{9... | collective-permute-start | bytes 1769480 | tf_op jit(solution)/shard_map/ppermute | solution.py:785
  190.4 32.6 %collective-permute-start.53 = (bf16[144,1024]{1,0:T(8,128)(2,1)S(1)}, bf16[144,1024]{1,0:T(8,128)(2,1)S(1)}, u32[]{:S(2)}, u32[]{:S(2)}) collective-permute-start(bf16[144,1024]{1,0:T(8,128)(2,1)S(1)} %get-tuple-element.270), channel_id=1, source_target_pairs={{0,4},{8,0},{16,8},{24,16},{28,24},{20,28},{12,20},{4,12},{1,5},{9... | collective-permute-start | bytes 884744 | tf_op jit(solution)/shard_map/ppermute | solution.py:785
  191.4 31.6 %collective-permute-start.54 = (bf16[144,1024]{1,0:T(8,128)(2,1)S(1)}, bf16[144,1024]{1,0:T(8,128)(2,1)S(1)}, u32[]{:S(2)}, u32[]{:S(2)}) collective-permute-start(bf16[144,1024]{1,0:T(8,128)(2,1)S(1)} %get-tuple-element.269), channel_id=1, source_target_pairs={{0,8},{8,16},{16,24},{24,28},{28,20},{20,12},{12,4},{4,0},{1,9},{9... | collective-permute-start | bytes 884744 | tf_op jit(solution)/shard_map/ppermute | solution.py:785
  204.5 18.6 %collective-permute-start.49 = (bf16[128,2304]{1,0:T(8,128)(2,1)S(1)}, bf16[128,2304]{1,0:T(8,128)(2,1)S(1)}, u32[]{:S(2)}, u32[]{:S(2)}) collective-permute-start(bf16[128,2304]{1,0:T(8,128)(2,1)S(1)} %get-tuple-element.273), channel_id=1, source_target_pairs={{0,4},{8,0},{16,8},{24,16},{28,24},{20,28},{12,20},{4,12},{1,5},{9... | collective-permute-start | bytes 1769480 | tf_op jit(solution)/shard_map/ppermute | solution.py:785
  205.4 17.7 %collective-permute-start.50 = (bf16[128,2304]{1,0:T(8,128)(2,1)S(1)}, bf16[128,2304]{1,0:T(8,128)(2,1)S(1)}, u32[]{:S(2)}, u32[]{:S(2)}) collective-permute-start(bf16[128,2304]{1,0:T(8,128)(2,1)S(1)} %get-tuple-element.274), channel_id=1, source_target_pairs={{0,8},{8,16},{16,24},{24,28},{28,20},{20,12},{12,4},{4,0},{1,9},{9... | collective-permute-start | bytes 1769480 | tf_op jit(solution)/shard_map/ppermute | solution.py:785
  206.6 16.5 %collective-permute-start.48 = (bf16[256,1024]{1,0:T(8,128)(2,1)S(1)}, bf16[256,1024]{1,0:T(8,128)(2,1)S(1)}, u32[]{:S(2)}, u32[]{:S(2)}) collective-permute-start(bf16[256,1024]{1,0:T(8,128)(2,1)S(1)} %add_convert_fusion.7), channel_id=1, source_target_pairs={{0,2},{1,3},{2,0},{3,1},{4,6},{5,7},{6,4},{7,5},{8,10},{9,11},{10,... | collective-permute-start | bytes 1572872 | tf_op jit(solution)/shard_map/ppermute | solution.py:744
  244.6 14.5 %collective-permute-start.61 = (bf16[256,1024]{1,0:T(8,128)(2,1)}, bf16[256,1024]{1,0:T(8,128)(2,1)}, u32[]{:S(2)}, u32[]{:S(2)}) collective-permute-start(bf16[256,1024]{1,0:T(8,128)(2,1)} %add_convert_fusion.5), channel_id=1, source_target_pairs={{0,2},{1,3},{2,0},{3,1},{4,6},{5,7},{6,4},{7,5},{8,10},{9,11},{10,... | collective-permute-start | bytes 1572872 | tf_op jit(solution)/shard_map/ppermute | solution.py:744
  (111 other events, 1056.9 us)
where the time goes:
time: 283 us; the launch traced here: 280 us
  Pallas kernels  87.3 us (31%)
  waiting for transfers between devices  65.1 us (23%)
  starting transfers between devices  63.3 us (22%)
  other arithmetic  36.2 us (13%)
  local copies, waits for them, and re-layouts  14 us (5%)
  matrix products  12.7 us (4%)
    pallas_call x7, Pallas kernels, call(): pl.pallas_call(kernel, out_shape=[jax.ShapeDtypeStruct(shape, kind) for s...  48 us
    ppermute x43, starting transfers between devices, ring_move(): lax.ppermute(values, 'dp', [(order[i], order[(i + step) % count]) for i i...  45.2 us
    ppermute x43, waiting for transfers between devices, ring_move(): lax.ppermute(values, 'dp', [(order[i], order[(i + step) % count]) for i i...  43.9 us
    pallas_call x5, Pallas kernels, block_call(): pl.pallas_call(kernel, out_shape=[jax.ShapeDtypeStruct(shape, kind) for s...  31.6 us
    ppermute x24, waiting for transfers between devices, swap(): return lax.ppermute(values, 'seq', [(i, i ^ bit) for i in range(count)])  19.7 us
    ppermute x24, starting transfers between devices, swap(): return lax.ppermute(values, 'seq', [(i, i ^ bit) for i in range(count)])  13.2 us
    dot_general x3, matrix products, dot(): lax.dot_general(left, right, (dims, ((), ())), preferred_element_type=F32)  12.7 us
    convert_element_type x8, other arithmetic, step(): sent = {way: value.astype(BF) for way, value in values.items()}  9.45 us
  transfers between devices with their start and end apart: 69, of which 29 were waited for; matrix products, arithmetic and copies ran while one was open for 17% of the time, Pallas kernels for 30%

commit v1 on v0

--- a/solution.py
+++ b/solution.py
@@ -287,19 +287,11 @@
             spot = pl.multiple_of((place ^ part) * columns, columns)
             sum_ref[:, pl.ds(spot, columns)] = total
 
-
-        def normalize(step, carry, piece=piece, index=index):
-            start = pl.multiple_of(step * BLOCK, BLOCK)
-            part = pl.ds(start, BLOCK)
-            values = sum_ref[part, :] + piece[part, :].astype(F32)
-            if index == 0:
-                here_ref[part, :] = values
-            factor = lax.rsqrt(jnp.mean(values * values, axis=-1, keepdims=True) + EPS)
-            target = pl.ds(pl.multiple_of(index * rows_each + start, BLOCK), BLOCK)
-            unit_ref[target, :] = (values * factor).astype(BF)
-            return carry
-
-        lax.fori_loop(0, rows_each // BLOCK, normalize, 0)
+        values = sum_ref[...] + piece[...].astype(F32)
+        if index == 0:
+            here_ref[...] = values
+        factor = lax.rsqrt(jnp.mean(values * values, axis=-1, keepdims=True) + EPS)
+        unit_ref[index * rows_each : (index + 1) * rows_each, :] = (values * factor).astype(BF)
 
 
 def hidden_kernel(offset_ref, unit_ref, *rest):
@@ -472,6 +464,13 @@
     lax.fori_loop(0, row_length // BLOCK, finish, 0)
 
 
+def as_column(values):
+    if values.shape[1] == 1:
+        return values
+    count = values.shape[1]
+    return jnp.transpose(jnp.broadcast_to(values, (count, count)))[:, :1]
+
+
 def attention_pack_kernel(
     place_ref,
     gain_ref,
@@ -483,7 +482,7 @@
     wide_ref,
     semaphore,
 ):
-    gain = gain_ref[...].astype(BF).astype(F32)
+    gain = as_column(gain_ref[...]).astype(BF).astype(F32)
     weights = (query_ref, key_ref, value_ref, output_ref)
     start = 0
     copies = []
@@ -954,7 +953,7 @@
         attention_pack_kernel,
         [((weight_rows, pack_width), BF)],
         1,
-        (place_array, gain_one),
+        (place_array, attention_gain[None, :] if weight_rows % PAIR == 0 else gain_one),
         58,
         pieces=(query_weight, key_weight, value_weight, output_weight),
         scratch=[pltpu.VMEM((weight_rows, pack_width), F32), pltpu.SemaphoreType.DMA((4,))],
@@ -1089,7 +1088,7 @@
     )
     hidden, gate_factor, up_factor = down_ring.step(hidden, gate_factor, up_factor)
     grad_rows = jnp.concatenate(grad_row_pieces)
-    down_scatter = ScatterRing([mm_tn(hidden, grad_rows)])
+    down_scatter = ScatterRing([mm_tn(hidden, grad_rows)], True)
     (down_scatter.terms,) = down_ring.step(down_scatter.terms)
     down_scatter.step()
     gate_up_grad, down_all = block_call(
@@ -1145,7 +1144,6 @@
         plain,
     )
     keep, send, branch_far = gate_up_scatter.step(keep, send, branch_far)
-    down_scatter.step(branch_far)
     branch_pieces = (branch, branch_near, branch_far, swap(branch_far, 1))
     half_sum, half_send = halves(keep, swap(send, 1))
     chunk_rows = query_width // (dp_count * seq_count)
@@ -1163,6 +1161,7 @@
         moved=8 * row_length * width,
     )
 
+    down_scatter.step(grad_mixed)
     grad_mixed, half_send = gate_up_scatter.step(grad_mixed, half_send)
     arrived = swap(half_send, 2)
     qkv_grad, gain_terms = call(

time: 283 us -> 282 us (level)
  other arithmetic: 36.2 us -> 39.8 us
    ppermute x24, waiting for transfers between devices: 19.7 us -> 13.8 us  [swap(): return lax.ppermute(values, 'seq', [(i, i ^ bit) for i in range(count)])]
    ppermute x43 -> x44, waiting for transfers between devices: 43.9 us -> 48.1 us  [ring_move(): lax.ppermute(values, 'dp', [(order[i], order[(i + step) % count]) for i i...]
    convert_element_type x8 -> x7, other arithmetic: 9.45 us -> 10.8 us  [step(): sent = {way: value.astype(BF) for way, value in values.items()}]
    ppermute x43 -> x44, starting transfers between devices: 45.2 us -> 45.4 us  [ring_move(): lax.ppermute(values, 'dp', [(order[i], order[(i + step) % count]) for i i...]
  transfers between devices with their start and end apart: 69 -> 70, of which waited for: 29 -> 31; matrix products, arithmetic and copies ran while one was open for 17% -> 19% of each run, Pallas kernels for 30% -> 29%
where the time goes in v1:
time: 282 us; the launch traced here: 279 us
  Pallas kernels  84.9 us (30%)
  waiting for transfers between devices  63.4 us (22%)
  starting transfers between devices  62.8 us (22%)
  other arithmetic  39.8 us (14%)
  matrix products  13.4 us (5%)
  local copies, waits for them, and re-layouts  13.3 us (5%)
    ppermute x44, waiting for transfers between devices, ring_move(): lax.ppermute(values, 'dp', [(order[i], order[(i + step) % count]) for i i...  48.1 us
    pallas_call x7, Pallas kernels, call(): pl.pallas_call(kernel, out_shape=[jax.ShapeDtypeStruct(shape, kind) for s...  46.5 us
    ppermute x44, starting transfers between devices, ring_move(): lax.ppermute(values, 'dp', [(order[i], order[(i + step) % count]) for i i...  45.4 us
    pallas_call x5, Pallas kernels, block_call(): pl.pallas_call(kernel, out_shape=[jax.ShapeDtypeStruct(shape, kind) for s...  30.9 us
    ppermute x24, waiting for transfers between devices, swap(): return lax.ppermute(values, 'seq', [(i, i ^ bit) for i in range(count)])  13.8 us
    dot_general x3, matrix products, dot(): lax.dot_general(left, right, (dims, ((), ())), preferred_element_type=F32)  13.4 us
    ppermute x24, starting transfers between devices, swap(): return lax.ppermute(values, 'seq', [(i, i ^ bit) for i in range(count)])  12.6 us
    convert_element_type x7, other arithmetic, step(): sent = {way: value.astype(BF) for way, value in values.items()}  10.8 us
  transfers between devices with their start and end apart: 70, of which 31 were waited for; matrix products, arithmetic and copies ran while one was open for 19% of the time, Pallas kernels for 29%

profile of v1, /device:TPU:0, one launch (start us, length us, event | category | flops | bytes accessed | tf_op | source)
XLA Modules:
  0.0 279.5 jit_solution(4629460955804169364)
XLA Ops:
  3.4 3.0 %collective-permute-start.1 = (bf16[128,768]{1,0:T(8,128)(2,1)}, bf16[128,768]{1,0:T(8,128)(2,1)}, u32[]{:S(2)}, u32[]{:S(2)}) collective-permute-start(bf16[128,768]{1,0:T(8,128)(2,1)} %shard_map.291.rest_0_), channel_id=1, source_target_pairs={{0,4},{8,0},{16,8},{24,16},{28,24},{20,28},{12,20},{4,12},{1,5},{9... | collective-permute-start | bytes 589832 | tf_op jit(solution)/shard_map/ppermute | solution.py:784
  15.1 3.0 %fusion.8 = (f32[1024,128]{1,0:T(8,128)}, f32[1024,128]{1,0:T(8,128)}) fusion(f32[128]{0:T(128)S(1)} %get-tuple-element.307, f32[128]{0:T(128)S(1)} %get-tuple-element.308, f32[1024]{0:T(1024)S(1)} %get-tuple-element.269), kind=kLoop, calls=%fused_computation.40 | loop fusion | flops 262144 | bytes 1053696 | tf_op jit(solution)/shard_map/mul | solution.py:63
  25.3 4.2 %shard_map.292.rest_0_ = bf16[128,2304]{1,0:T(8,128)(2,1)} custom-call(s32[1]{0:T(128)} %bitcast.place_ref, f32[128,1]{1,0:T(8,128)} %copy.37.gain_ref, f32[128,4608]{1,0:T(8,128)} %gate_ref.3, f32[128,4608]{1,0:T(8,128)} %up_ref.3), custom_call_target="tpu_custom_call" | custom-call | flops 2415000064 | tf_op jit(solution)/shard_map/pallas_call | solution.py:676
  32.4 4.8 %collective-permute-done.9.rest_7_ = bf16[128,768]{1,0:T(8,128)(2,1)S(1)} collective-permute-done((bf16[128,768]{1,0:T(8,128)(2,1)S(1)}, bf16[128,768]{1,0:T(8,128)(2,1)S(1)}, u32[]{:S(2)}, u32[]{:S(2)}) %collective-permute-start.9) | collective-permute-done | bytes 196640 | tf_op jit(solution)/shard_map/ppermute | solution.py:784
  43.2 9.0 %shard_map.293 = (bf16[1024,1024]{1,0:T(8,128)(2,1)}, f32[1024,384]{1,0:T(8,128)}, bf16[1024,256]{1,0:T(8,128)(2,1)}, bf16[1024,256]{1,0:T(8,128)(2,1)}, bf16[10...) custom-call(s32[1]{0:T(128)} %bitcast.place_ref, s32[8]{0:T(128)} %fusion.22.offset_ref, bf16[256,1024]{1,0:T(8,128)(2,1)} %bitcast.43, ...), custom_call_target="tpu_custom_call" | custom-call | flops 5462499840 | tf_op jit(solution)/shard_map/pallas_call | solution.py:676
  56.1 7.1 %shard_map.295.o0_ref.mixed_ref = bf16[1024,256]{1,0:T(8,128)(2,1)} custom-call(s32[8]{0:T(128)} %slice.147.low_ref, bf16[1024,256]{1,0:T(8,128)(2,1)} %get-tuple-element.164.query_ref, bf16[1024,256]{1,0:T(8,128)(2,1)} %get-tuple-element.165.key_ref, bf16[1024,256]{1,0:T(8,128)(2,1)} %get-tuple-element.166.value_ref, ...), custom_call_target="tpu_custom_call" | custom-call | flops 4024999936 | tf_op jit(solution)/shard_map/pallas_call | solution.py:676
  70.3 3.1 %collective-permute-done.19.o2_ref = bf16[1024,256]{1,0:T(8,128)(2,1)} collective-permute-done((bf16[1024,256]{1,0:T(8,128)(2,1)}, bf16[1024,256]{1,0:T(8,128)(2,1)}, u32[]{:S(2)}, u32[]{:S(2)}) %collective-permute-start.19) | collective-permute-done | bytes 524320 | tf_op jit(solution)/shard_map/ppermute | solution.py:743
  73.4 4.5 %collective-permute-done.17.rest_6_ = bf16[128,2304]{1,0:T(8,128)(2,1)S(1)} collective-permute-done((bf16[128,2304]{1,0:T(8,128)(2,1)}, bf16[128,2304]{1,0:T(8,128)(2,1)S(1)}, u32[]{:S(2)}, u32[]{:S(2)}) %collective-permute-start.17) | collective-permute-done | bytes 589856 | tf_op jit(solution)/shard_map/ppermute | solution.py:784
  86.3 5.1 %shard_map.296 = (bf16[1024,1024]{1,0:T(8,128)(2,1)S(1)}, f32[256,1024]{1,0:T(8,128)S(1)}) custom-call(s32[1]{0:T(128)} %bitcast.place_ref, bf16[256,1024]{1,0:T(8,128)(2,1)S(1)} %bitcast.46, bf16[256,1024]{1,0:T(8,128)(2,1)} %collective-permute-done.x1_ref, bf16[256,1024]{1,0:T(8,128)(2,1)} %collective-permute-done.5.x2_ref, ...), custom_call_target="tpu_custom_call" | custom-call | flops 2875000064 | tf_op jit(solution)/shard_map/pallas_call | solution.py:676
  93.5 3.1 %collective-permute-done.26.rest_7_ = bf16[128,2304]{1,0:T(8,128)(2,1)S(1)} collective-permute-done((bf16[128,2304]{1,0:T(8,128)(2,1)}, bf16[128,2304]{1,0:T(8,128)(2,1)S(1)}, u32[]{:S(2)}, u32[]{:S(2)}) %collective-permute-start.26) | collective-permute-done | bytes 589856 | tf_op jit(solution)/shard_map/ppermute | solution.py:784
  96.6 8.7 %shard_map.297 = (bf16[1024,1152]{1,0:T(8,128)(2,1)S(1)}, bf16[1024,1152]{1,0:T(8,128)(2,1)S(1)}, bf16[1024,1152]{1,0:T(8,128)(2,1)S(1)}) custom-call(s32[8]{0:T(128)S(1)} %copy-done.22, bf16[1024,1024]{1,0:T(8,128)(2,1)S(1)} %get-tuple-element.204.unit_ref, bf16[128,2304]{1,0:T(8,128)(2,1)S(1)} %copy-done.12, ...), custom_call_target="tpu_custom_call" | custom-call | flops 5175000064 | tf_op jit(solution)/shard_map/pallas_call | solution.py:690
  107.4 4.3 %fusion.26 = f32[1152,1024]{1,0:T(8,128)S(1)} fusion(bf16[1024,1152]{1,0:T(8,128)(2,1)S(1)} %get-tuple-element.208.left_ref, bf16[256,1024]{1,0:T(8,128)(2,1)} %collective-permute-done.30, bf16[256,1024]{1,0:T(8,128)(2,1)} %collective-permute-done.10, bf16[256,1024]{1,0:T(8,128)(2,1)} %collective-permute-done.29, bf16[256,1024]{1,0:T(8,128)(2,1)} %bitcast.9), kind=kOutput, calls=%fused_computation.119 | convolution fusion | flops 2424307712 | bytes 9175040 | tf_op jit(solution)/shard_map/dot_general | solution.py:23
  117.9 3.8 %collective-permute-done.33.rest_6_ = bf16[144,1024]{1,0:T(8,128)(2,1)S(1)} collective-permute-done((bf16[144,1024]{1,0:T(8,128)(2,1)S(1)}, bf16[144,1024]{1,0:T(8,128)(2,1)S(1)}, u32[]{:S(2)}, u32[]{:S(2)}) %collective-permute-start.33) | collective-permute-done | bytes 294944 | tf_op jit(solution)/shard_map/ppermute | solution.py:784
  122.6 4.9 %shard_map.298 = (bf16[1024,2304]{1,0:T(8,128)(2,1)S(1)}, bf16[1152,1024]{1,0:T(8,128)(2,1)S(1)}) custom-call(s32[8]{0:T(128)S(1)} %fusion.23.offset_ref, bf16[1024,1024]{1,0:T(8,128)(2,1)S(1)} %pad_maximum_fusion.1.grad_ref, bf16[1024,1152]{1,0:T(8,128)(2,1)S(1)} %get-tuple-element.192.gate_factor_ref, ...), custom_call_target="tpu_custom_call" | custom-call | flops 3104999936 | tf_op jit(solution)/shard_map/pallas_call | solution.py:690
  129.9 9.2 %shard_map.299 = (f32[512,1024]{1,0:T(8,128)S(1)}, bf16[512,1024]{1,0:T(8,128)(2,1)}) custom-call(s32[4]{0:T(128)S(1)} %iota.55.order_ref, s32[8]{0:T(128)S(1)} %copy-done.22, bf16[1024,2304]{1,0:T(8,128)(2,1)S(1)} %get-tuple-element.199.left_ref, bf16[128,2304]{1,0:T(8,128)(2,1)S(1)} %copy-done.12, bf16[128,2304]{1,0:T(8,128)(2,1)} %collective-permute-done.12.rest_1_, ...), custom_call_target="tpu_custom_call" | custom-call | flops 5844113920 | tf_op jit(solution)/shard_map/pallas_call | solution.py:690
  140.0 2.8 %collective-permute-done.37 = bf16[512,1024]{1,0:T(8,128)(2,1)} collective-permute-done((bf16[512,1024]{1,0:T(8,128)(2,1)}, bf16[512,1024]{1,0:T(8,128)(2,1)}, u32[]{:S(2)}, u32[]{:S(2)}) %collective-permute-start.37) | collective-permute-done | bytes 1048608 | tf_op jit(solution)/shard_map/ppermute | solution.py:743
  145.3 7.7 %convolution_convert_fusion = bf16[1024,2304]{1,0:T(8,128)(2,1)S(1)} fusion(bf16[1024,1024]{1,0:T(8,128)(2,1)S(1)} %copy-done.28, bf16[1024,2304]{1,0:T(8,128)(2,1)} %copy-done.24), kind=kOutput, calls=%fused_computation | convolution fusion | flops 4834197504 | bytes 11534336 | tf_op jit(solution)/shard_map/dot_general | solution.py:23
  171.9 4.3 %shard_map.300 = (f32[512,1024]{1,0:T(8,128)S(1)}, bf16[512,1024]{1,0:T(8,128)(2,1)S(1)}) custom-call(s32[4]{0:T(128)S(1)} %iota.56.order_ref, s32[1]{0:T(128)} %constant.399.clone.1.offset_ref, bf16[1024,1152]{1,0:T(8,128)(2,1)S(1)} %copy-done.31, bf16[1152,1024]{1,0:T(8,128)(2,1)S(1)} %copy-done.26), custom_call_target="tpu_custom_call" | custom-call | flops 3065806848 | tf_op jit(solution)/shard_map/pallas_call | solution.py:690
  184.9 2.8 %shard_map.301 = (bf16[1024,256]{1,0:T(8,128)(2,1)S(1)}, f32[512,512]{1,0:T(8,128)S(1)}) custom-call(s32[1]{0:T(128)} %bitcast.place_ref, bf16[256,1024]{1,0:T(8,128)(2,1)S(1)} %copy-done.7, bf16[256,1024]{1,0:T(8,128)(2,1)S(1)} %collective-permute-done.47.g1_ref, bf16[256,1024]{1,0:T(8,128)(2,1)S(1)} %collective-permute-done.43.g2_ref, ...), custom_call_target="tpu_custom_call" | custom-call | flops 1724999936 | tf_op jit(solution)/shard_map/pallas_call | solution.py:676
  191.6 7.5 %collective-permute-done.45 = bf16[128,2304]{1,0:T(8,128)(2,1)S(1)} collective-permute-done((bf16[128,2304]{1,0:T(8,128)(2,1)S(1)}, bf16[128,2304]{1,0:T(8,128)(2,1)S(1)}, u32[]{:S(2)}, u32[]{:S(2)}) %collective-permute-start.45) | collective-permute-done | bytes 589856 | tf_op jit(solution)/shard_map/ppermute | solution.py:784
  205.3 15.7 %shard_map.302 = (bf16[1024,512]{1,0:T(8,128)(2,1)S(1)}, f32[8,128]{1,0:T(8,128)S(1)}) custom-call(s32[8]{0:T(128)S(1)} %copy-done.23, bf16[1024,256]{1,0:T(8,128)(2,1)S(1)} %get-tuple-element.221.grad_ref, bf16[1024,256]{1,0:T(8,128)(2,1)S(1)} %copy-done.33, bf16[1024,256]{1,0:T(8,128)(2,1)S(1)} %copy-done.34, bf16[1024,256]{1,0:T(8,128)(2,1)S(1)} %copy-done.35, ...), custom_call_target="tpu_custom_call" | custom-call | flops 8970000384 | tf_op jit(solution)/shard_map/pallas_call | solution.py:676
  226.4 3.9 %shard_map.303 = (f32[512,1024]{1,0:T(8,128)S(1)}, bf16[512,1024]{1,0:T(8,128)(2,1)}) custom-call(s32[4]{0:T(128)S(1)} %iota_xor_fusion.order_ref, s32[1]{0:T(128)} %constant.399.clone.1.offset_ref, bf16[1024,512]{1,0:T(8,128)(2,1)S(1)} %get-tuple-element.239.left_ref, bf16[1024,512]{1,0:T(8,128)(2,1)S(1)} %copy-done.29), custom_call_target="tpu_custom_call" | custom-call | flops 1522303104 | tf_op jit(solution)/shard_map/pallas_call | solution.py:690
  253.3 4.2 %all-to-all-start = ((bf16[4,32,2304]{2,1,0:T(8,128)(2,1)}), bf16[4,32,2304]{2,1,0:T(8,128)(2,1)}, u32[]{:S(2)}, u32[]{:S(2)}) async-start(bf16[4,32,2304]{2,1,0:T(8,128)(2,1)} %bitcast.53), calls=%async_computation | async-start | bytes 1179648 | tf_op jit(solution)/shard_map/all_to_all | solution.py:1208
  267.1 3.0 %shard_map.305 = (f32[32,4608]{1,0:T(8,128)}, f32[32,4608]{1,0:T(8,128)}, f32[1,32]{1,0:T(1,128)}) custom-call(s32[1]{0:T(128)} %bitcast.place_ref, bf16[4,32,2304]{2,1,0:T(8,128)(2,1)} %all-to-all-done.sums_ref, f32[128,4608]{1,0:T(8,128)} %gate_ref.3, f32[128,4608]{1,0:T(8,128)} %up_ref.3, f32[128,1]{1,0:T(8,128)} %copy.39.gain_ref), custom_call_target="tpu_custom_call" | custom-call | flops 1782499968 | tf_op jit(solution)/shard_map/pallas_call | solution.py:626
  (349 shorter events, 148.0 us)
Async XLA Ops:
  6.5 14.0 %collective-permute-start.5 = (bf16[256,1024]{1,0:T(8,128)(2,1)S(1)}, bf16[256,1024]{1,0:T(8,128)(2,1)}, u32[]{:S(2)}, u32[]{:S(2)}) collective-permute-start(bf16[256,1024]{1,0:T(8,128)(2,1)S(1)} %bitcast.44), channel_id=1, source_target_pairs={{0,2},{1,3},{2,0},{3,1},{4,6},{5,7},{6,4},{7,5},{8,10},{9,11},{10,... | collective-permute-start | bytes 1572872 | tf_op jit(solution)/shard_map/ppermute | solution.py:743
  20.5 16.6 %collective-permute-start.10 = (bf16[256,1024]{1,0:T(8,128)(2,1)}, bf16[256,1024]{1,0:T(8,128)(2,1)}, u32[]{:S(2)}, u32[]{:S(2)}) collective-permute-start(bf16[256,1024]{1,0:T(8,128)(2,1)} %bitcast.9), channel_id=1, source_target_pairs={{0,2},{1,3},{2,0},{3,1},{4,6},{5,7},{6,4},{7,5},{8,10},{9,11},{10,... | collective-permute-start | bytes 1572872 | tf_op jit(solution)/shard_map/ppermute | solution.py:743
  22.0 20.4 %collective-permute-start = (bf16[256,1024]{1,0:T(8,128)(2,1)S(1)}, bf16[256,1024]{1,0:T(8,128)(2,1)}, u32[]{:S(2)}, u32[]{:S(2)}) collective-permute-start(bf16[256,1024]{1,0:T(8,128)(2,1)S(1)} %bitcast.45), channel_id=1, source_target_pairs={{0,1},{1,0},{2,3},{3,2},{4,5},{5,4},{6,7},{7,6},{8,9},{9,8},{10,11... | collective-permute-start | bytes 1572872 | tf_op jit(solution)/shard_map/ppermute | solution.py:743
  22.8 19.6 %collective-permute-start.6 = (bf16[256,1024]{1,0:T(8,128)(2,1)}, bf16[256,1024]{1,0:T(8,128)(2,1)S(1)}, u32[]{:S(2)}, u32[]{:S(2)}) collective-permute-start(bf16[256,1024]{1,0:T(8,128)(2,1)} %collective-permute-done.5.x2_ref), channel_id=1, source_target_pairs={{0,1},{1,0},{2,3},{3,2},{4,5},{5,4},{6,7},{7,6},{8,9},{9,8},{10,11... | collective-permute-start | bytes 1572872 | tf_op jit(solution)/shard_map/ppermute | solution.py:743
  37.1 16.3 %collective-permute-start.11 = (bf16[128,2304]{1,0:T(8,128)(2,1)}, bf16[128,2304]{1,0:T(8,128)(2,1)S(1)}, u32[]{:S(2)}, u32[]{:S(2)}) collective-permute-start(bf16[128,2304]{1,0:T(8,128)(2,1)} %shard_map.292.rest_0_), channel_id=1, source_target_pairs={{0,4},{8,0},{16,8},{24,16},{28,24},{20,28},{12,20},{4,12},{1,5},{9... | collective-permute-start | bytes 1769480 | tf_op jit(solution)/shard_map/ppermute | solution.py:784
  38.7 14.8 %collective-permute-start.12 = (bf16[128,2304]{1,0:T(8,128)(2,1)}, bf16[128,2304]{1,0:T(8,128)(2,1)}, u32[]{:S(2)}, u32[]{:S(2)}) collective-permute-start(bf16[128,2304]{1,0:T(8,128)(2,1)} %shard_map.292.rest_0_), channel_id=1, source_target_pairs={{0,8},{8,16},{16,24},{24,28},{28,20},{20,12},{12,4},{4,0},{1,9},{9... | collective-permute-start | bytes 1769480 | tf_op jit(solution)/shard_map/ppermute | solution.py:784
  55.1 12.7 %collective-permute-start.16 = (bf16[128,2304]{1,0:T(8,128)(2,1)}, bf16[128,2304]{1,0:T(8,128)(2,1)}, u32[]{:S(2)}, u32[]{:S(2)}) collective-permute-start(bf16[128,2304]{1,0:T(8,128)(2,1)} %collective-permute-done.12.rest_1_), channel_id=1, source_target_pairs={{0,8},{8,16},{16,24},{24,28},{28,20},{20,12},{12,4},{4,0},{1,9},{9... | collective-permute-start | bytes 1769480 | tf_op jit(solution)/shard_map/ppermute | solution.py:784
  80.1 16.5 %collective-permute-start.26 = (bf16[128,2304]{1,0:T(8,128)(2,1)}, bf16[128,2304]{1,0:T(8,128)(2,1)S(1)}, u32[]{:S(2)}, u32[]{:S(2)}) collective-permute-start(bf16[128,2304]{1,0:T(8,128)(2,1)} %collective-permute-done.18.rest_5_), channel_id=1, source_target_pairs={{0,8},{8,16},{16,24},{24,28},{28,20},{20,12},{12,4},{4,0},{1,9},{9... | collective-permute-start | bytes 1769480 | tf_op jit(solution)/shard_map/ppermute | solution.py:784
  91.4 13.9 %collective-permute-start.24 = (bf16[144,1024]{1,0:T(8,128)(2,1)S(1)}, bf16[144,1024]{1,0:T(8,128)(2,1)S(1)}, u32[]{:S(2)}, u32[]{:S(2)}) collective-permute-start(bf16[144,1024]{1,0:T(8,128)(2,1)S(1)} %collective-permute-done.23.rest_1_), channel_id=1, source_target_pairs={{0,4},{8,0},{16,8},{24,16},{28,24},{20,28},{12,20},{4,12},{1,5},{9... | collective-permute-start | bytes 884744 | tf_op jit(solution)/shard_map/ppermute | solution.py:784
  92.6 12.7 %collective-permute-start.25 = (bf16[144,1024]{1,0:T(8,128)(2,1)S(1)}, bf16[144,1024]{1,0:T(8,128)(2,1)S(1)}, u32[]{:S(2)}, u32[]{:S(2)}) collective-permute-start(bf16[144,1024]{1,0:T(8,128)(2,1)S(1)} %dynamic-slice_convert_fusion.1.rest_0_), channel_id=1, source_target_pairs={{0,8},{8,16},{16,24},{24,28},{28,20},{20,12},{12,4},{4,0},{1,9},{9... | collective-permute-start | bytes 884744 | tf_op jit(solution)/shard_map/ppermute | solution.py:784
  144.0 14.0 %collective-permute-start.40 = (bf16[256,1024]{1,0:T(8,128)(2,1)S(1)}, bf16[256,1024]{1,0:T(8,128)(2,1)S(1)}, u32[]{:S(2)}, u32[]{:S(2)}) collective-permute-start(bf16[256,1024]{1,0:T(8,128)(2,1)S(1)} %add_convert_fusion.8), channel_id=1, source_target_pairs={{0,2},{1,3},{2,0},{3,1},{4,6},{5,7},{6,4},{7,5},{8,10},{9,11},{10,... | collective-permute-start | bytes 1572872 | tf_op jit(solution)/shard_map/ppermute | solution.py:743
  163.7 16.4 %collective-permute-start.42 = (bf16[128,2304]{1,0:T(8,128)(2,1)S(1)}, bf16[128,2304]{1,0:T(8,128)(2,1)}, u32[]{:S(2)}, u32[]{:S(2)}) collective-permute-start(bf16[128,2304]{1,0:T(8,128)(2,1)S(1)} %pad_maximum_fusion.3), channel_id=1, source_target_pairs={{0,8},{8,16},{16,24},{24,28},{28,20},{20,12},{12,4},{4,0},{1,9},{9... | collective-permute-start | bytes 1769480 | tf_op jit(solution)/shard_map/ppermute | solution.py:784
  164.0 16.4 %collective-permute-start.41 = (bf16[128,2304]{1,0:T(8,128)(2,1)S(1)}, bf16[128,2304]{1,0:T(8,128)(2,1)}, u32[]{:S(2)}, u32[]{:S(2)}) collective-permute-start(bf16[128,2304]{1,0:T(8,128)(2,1)S(1)} %pad_maximum_fusion.2), channel_id=1, source_target_pairs={{0,4},{8,0},{16,8},{24,16},{28,24},{20,28},{12,20},{4,12},{1,5},{9... | collective-permute-start | bytes 1769480 | tf_op jit(solution)/shard_map/ppermute | solution.py:784
  168.1 19.7 %collective-permute-start.52 = (bf16[144,1024]{1,0:T(8,128)(2,1)S(1)}, bf16[144,1024]{1,0:T(8,128)(2,1)S(1)}, u32[]{:S(2)}, u32[]{:S(2)}) collective-permute-start(bf16[144,1024]{1,0:T(8,128)(2,1)S(1)} %get-tuple-element.274), channel_id=1, source_target_pairs={{0,4},{8,0},{16,8},{24,16},{28,24},{20,28},{12,20},{4,12},{1,5},{9... | collective-permute-start | bytes 884744 | tf_op jit(solution)/shard_map/ppermute | solution.py:784
  169.4 18.4 %collective-permute-start.53 = (bf16[144,1024]{1,0:T(8,128)(2,1)S(1)}, bf16[144,1024]{1,0:T(8,128)(2,1)S(1)}, u32[]{:S(2)}, u32[]{:S(2)}) collective-permute-start(bf16[144,1024]{1,0:T(8,128)(2,1)S(1)} %get-tuple-element.273), channel_id=1, source_target_pairs={{0,8},{8,16},{16,24},{24,28},{28,20},{20,12},{12,4},{4,0},{1,9},{9... | collective-permute-start | bytes 884744 | tf_op jit(solution)/shard_map/ppermute | solution.py:784
  182.9 16.2 %collective-permute-start.45 = (bf16[128,2304]{1,0:T(8,128)(2,1)S(1)}, bf16[128,2304]{1,0:T(8,128)(2,1)S(1)}, u32[]{:S(2)}, u32[]{:S(2)}) collective-permute-start(bf16[128,2304]{1,0:T(8,128)(2,1)S(1)} %get-tuple-element.278), channel_id=1, source_target_pairs={{0,4},{8,0},{16,8},{24,16},{28,24},{20,28},{12,20},{4,12},{1,5},{9... | collective-permute-start | bytes 1769480 | tf_op jit(solution)/shard_map/ppermute | solution.py:784
  184.7 16.2 %collective-permute-start.46 = (bf16[128,2304]{1,0:T(8,128)(2,1)S(1)}, bf16[128,2304]{1,0:T(8,128)(2,1)S(1)}, u32[]{:S(2)}, u32[]{:S(2)}) collective-permute-start(bf16[128,2304]{1,0:T(8,128)(2,1)S(1)} %get-tuple-element.277), channel_id=1, source_target_pairs={{0,8},{8,16},{16,24},{24,28},{28,20},{20,12},{12,4},{4,0},{1,9},{9... | collective-permute-start | bytes 1769480 | tf_op jit(solution)/shard_map/ppermute | solution.py:784
  189.2 31.8 %collective-permute-start.54 = (bf16[144,1024]{1,0:T(8,128)(2,1)S(1)}, bf16[144,1024]{1,0:T(8,128)(2,1)S(1)}, u32[]{:S(2)}, u32[]{:S(2)}) collective-permute-start(bf16[144,1024]{1,0:T(8,128)(2,1)S(1)} %get-tuple-element.272), channel_id=1, source_target_pairs={{0,4},{8,0},{16,8},{24,16},{28,24},{20,28},{12,20},{4,12},{1,5},{9... | collective-permute-start | bytes 884744 | tf_op jit(solution)/shard_map/ppermute | solution.py:784
  191.1 29.9 %collective-permute-start.55 = (bf16[144,1024]{1,0:T(8,128)(2,1)S(1)}, bf16[144,1024]{1,0:T(8,128)(2,1)S(1)}, u32[]{:S(2)}, u32[]{:S(2)}) collective-permute-start(bf16[144,1024]{1,0:T(8,128)(2,1)S(1)} %get-tuple-element.271), channel_id=1, source_target_pairs={{0,8},{8,16},{16,24},{24,28},{28,20},{20,12},{12,4},{4,0},{1,9},{9... | collective-permute-start | bytes 884744 | tf_op jit(solution)/shard_map/ppermute | solution.py:784
  202.4 18.6 %collective-permute-start.50 = (bf16[128,2304]{1,0:T(8,128)(2,1)S(1)}, bf16[128,2304]{1,0:T(8,128)(2,1)S(1)}, u32[]{:S(2)}, u32[]{:S(2)}) collective-permute-start(bf16[128,2304]{1,0:T(8,128)(2,1)S(1)} %get-tuple-element.275), channel_id=1, source_target_pairs={{0,4},{8,0},{16,8},{24,16},{28,24},{20,28},{12,20},{4,12},{1,5},{9... | collective-permute-start | bytes 1769480 | tf_op jit(solution)/shard_map/ppermute | solution.py:784
  203.2 17.8 %collective-permute-start.51 = (bf16[128,2304]{1,0:T(8,128)(2,1)S(1)}, bf16[128,2304]{1,0:T(8,128)(2,1)S(1)}, u32[]{:S(2)}, u32[]{:S(2)}) collective-permute-start(bf16[128,2304]{1,0:T(8,128)(2,1)S(1)} %get-tuple-element.276), channel_id=1, source_target_pairs={{0,8},{8,16},{16,24},{24,28},{28,20},{20,12},{12,4},{4,0},{1,9},{9... | collective-permute-start | bytes 1769480 | tf_op jit(solution)/shard_map/ppermute | solution.py:784
  204.5 16.5 %collective-permute-start.49 = (bf16[256,1024]{1,0:T(8,128)(2,1)S(1)}, bf16[256,1024]{1,0:T(8,128)(2,1)S(1)}, u32[]{:S(2)}, u32[]{:S(2)}) collective-permute-start(bf16[256,1024]{1,0:T(8,128)(2,1)S(1)} %add_convert_fusion.7), channel_id=1, source_target_pairs={{0,2},{1,3},{2,0},{3,1},{4,6},{5,7},{6,4},{7,5},{8,10},{9,11},{10,... | collective-permute-start | bytes 1572872 | tf_op jit(solution)/shard_map/ppermute | solution.py:743
  243.9 14.3 %collective-permute-start.62 = (bf16[256,1024]{1,0:T(8,128)(2,1)}, bf16[256,1024]{1,0:T(8,128)(2,1)}, u32[]{:S(2)}, u32[]{:S(2)}) collective-permute-start(bf16[256,1024]{1,0:T(8,128)(2,1)} %add_convert_fusion.5), channel_id=1, source_target_pairs={{0,2},{1,3},{2,0},{3,1},{4,6},{5,7},{6,4},{7,5},{8,10},{9,11},{10,... | collective-permute-start | bytes 1572872 | tf_op jit(solution)/shard_map/ppermute | solution.py:743
  253.3 13.8 %all-to-all-start = ((bf16[4,32,2304]{2,1,0:T(8,128)(2,1)}), bf16[4,32,2304]{2,1,0:T(8,128)(2,1)}, u32[]{:S(2)}, u32[]{:S(2)}) async-start(bf16[4,32,2304]{2,1,0:T(8,128)(2,1)} %bitcast.53), calls=%async_computation | async-start | bytes 1179648 | tf_op jit(solution)/shard_map/all_to_all | solution.py:1208
  (112 other events, 1019.9 us)

commit v2 on v1

--- a/solution.py
+++ b/solution.py
@@ -1162,24 +1162,20 @@
     )
 
     down_scatter.step(grad_mixed)
-    grad_mixed, half_send = gate_up_scatter.step(grad_mixed, half_send)
+    grad_mixed, half_send = lax.optimization_barrier((grad_mixed, half_send))
     arrived = swap(half_send, 2)
     qkv_grad, gain_terms = call(
         functools.partial(back_kernel, head_dim),
         [((row_length, qkv_width), BF), ((8, PAIR), F32)],
         1,
-        (block_lows, after(grad_mixed, gate_up_scatter.sent), queries, keys_two, values_two, raw)
+        (block_lows, grad_mixed, queries, keys_two, values_two, raw)
         + (cos_wide, sin_wide, head_gains, row_starts, usable),
         24,
         scratch=[pltpu.VMEM((row_length, 2 * key_here), F32)] * 2,
         flops=4 * row_length * width * qkv_width,
         moved=12 * row_length * width,
     )
-    qkv_grad, gain_terms, arrived, gate_up_arrived, down_arrived = lax.optimization_barrier(
-        (qkv_grad, gain_terms, arrived, gate_up_scatter.arrived(), down_scatter.arrived())
-    )
-    down_scatter.take(down_arrived)
-    gate_up_scatter.take(gate_up_arrived)
+    qkv_grad, gain_terms, arrived = gate_up_scatter.step(qkv_grad, gain_terms, arrived)
     layer_out = (after_here + half_sum + arrived.astype(F32)).astype(BF)
     gain_rows = jnp.concatenate([gain_terms[0:1], gain_terms[1:2]], axis=1)
     gain_rows = jnp.pad(gain_rows, ((0, 15), (0, qkv_width - 2 * PAIR)))
@@ -1193,10 +1189,8 @@
     )
     attention_scatter = ScatterRing([packed.reshape(-1, qkv_width)])
     attention_scatter.step()
-    gate_up_scatter.take(after(gate_up_scatter.arrived(), attention_scatter.sent))
-    gate_up_sums = gate_up_scatter.result().astype(BF)
     keep, send = split_product(
-        after(qkv_grad, gate_up_sums),
+        after(qkv_grad, attention_scatter.sent),
         (width, qkv_width),
         jnp.zeros((1,), jnp.int32),
         [qkv_weight],
@@ -1204,13 +1198,14 @@
         order,
     )
     keep, send = attention_scatter.step(keep, send)
-    gate_up_sums = after(gate_up_sums, attention_scatter.sent)
+    gate_up_scatter.take(after(gate_up_scatter.arrived(), attention_scatter.arrived()))
+    gate_up_sums = gate_up_scatter.result().astype(BF)
     hidden_own = lax.all_to_all(
         gate_up_sums.reshape(seq_count, own_rows, -1), "seq", split_axis=0, concat_axis=0, tiled=True
     )
     half_sum, half_send = halves(keep, swap(send, 1))
-    (half_send,) = attention_scatter.step(half_send)
     arrived = swap(half_send, 2)
+    attention_scatter.step(half_send)
     for _ in range(attention_scatter.steps - 3):
         (arrived,) = attention_scatter.step(arrived)
         hidden_own = after(hidden_own, attention_scatter.sent)

time: 282 us -> 279 us (0.989)
  other arithmetic: 39.8 us -> 35.1 us
    unnamed x132 -> x118, local copies, waits for them, and re-layouts: 7.78 us -> 8.73 us
  transfers between devices with their start and end apart: 70 -> 70, of which waited for: 31 -> 32; matrix products, arithmetic and copies ran while one was open for 19% -> 17% of each run, Pallas kernels for 29% -> 30%
where the time goes in v2:
time: 279 us; the launch traced here: 274 us
  Pallas kernels  83.7 us (30%)
  starting transfers between devices  64.3 us (23%)
  waiting for transfers between devices  62.6 us (22%)
  other arithmetic  35.1 us (13%)
  local copies, waits for them, and re-layouts  13.6 us (5%)
  matrix products  13.4 us (5%)
    ppermute x44, waiting for transfers between devices, ring_move(): lax.ppermute(values, 'dp', [(order[i], order[(i + step) % count]) for i i...  48.7 us
    pallas_call x7, Pallas kernels, call(): pl.pallas_call(kernel, out_shape=[jax.ShapeDtypeStruct(shape, kind) for s...  46.4 us
    ppermute x44, starting transfers between devices, ring_move(): lax.ppermute(values, 'dp', [(order[i], order[(i + step) % count]) for i i...  46.3 us
    pallas_call x5, Pallas kernels, block_call(): pl.pallas_call(kernel, out_shape=[jax.ShapeDtypeStruct(shape, kind) for s...  29.8 us
    ppermute x24, waiting for transfers between devices, swap(): return lax.ppermute(values, 'seq', [(i, i ^ bit) for i in range(count)])  13.8 us
    dot_general x3, matrix products, dot(): lax.dot_general(left, right, (dims, ((), ())), preferred_element_type=F32)  13.4 us
    ppermute x24, starting transfers between devices, swap(): return lax.ppermute(values, 'seq', [(i, i ^ bit) for i in range(count)])  13.2 us
    convert_element_type x7, other arithmetic, step(): sent = {way: value.astype(BF) for way, value in values.items()}  9.69 us
  transfers between devices with their start and end apart: 70, of which 32 were waited for; matrix products, arithmetic and copies ran while one was open for 17% of the time, Pallas kernels for 30%

profile of v2, /device:TPU:0, one launch (start us, length us, event | category | flops | bytes accessed | tf_op | source)
XLA Modules:
  0.0 274.4 jit_solution(17753973728605890267)
XLA Ops:
  3.4 3.0 %collective-permute-start.1 = (bf16[128,768]{1,0:T(8,128)(2,1)}, bf16[128,768]{1,0:T(8,128)(2,1)}, u32[]{:S(2)}, u32[]{:S(2)}) collective-permute-start(bf16[128,768]{1,0:T(8,128)(2,1)} %shard_map.291.rest_0_), channel_id=1, source_target_pairs={{0,4},{8,0},{16,8},{24,16},{28,24},{20,28},{12,20},{4,12},{1,5},{9... | collective-permute-start | bytes 589832 | tf_op jit(solution)/shard_map/ppermute | solution.py:784
  15.1 3.0 %fusion.8 = (f32[1024,128]{1,0:T(8,128)}, f32[1024,128]{1,0:T(8,128)}) fusion(f32[128]{0:T(128)S(1)} %get-tuple-element.293, f32[128]{0:T(128)S(1)} %get-tuple-element.294, f32[1024]{0:T(1024)S(1)} %get-tuple-element.255), kind=kLoop, calls=%fused_computation.40 | loop fusion | flops 262144 | bytes 1053696 | tf_op jit(solution)/shard_map/mul | solution.py:63
  25.3 4.2 %shard_map.292.rest_0_ = bf16[128,2304]{1,0:T(8,128)(2,1)} custom-call(s32[1]{0:T(128)} %bitcast.place_ref, f32[128,1]{1,0:T(8,128)} %copy.37.gain_ref, f32[128,4608]{1,0:T(8,128)} %gate_ref.3, f32[128,4608]{1,0:T(8,128)} %up_ref.3), custom_call_target="tpu_custom_call" | custom-call | flops 2415000064 | tf_op jit(solution)/shard_map/pallas_call | solution.py:676
  32.4 4.8 %collective-permute-done.9.rest_7_ = bf16[128,768]{1,0:T(8,128)(2,1)S(1)} collective-permute-done((bf16[128,768]{1,0:T(8,128)(2,1)S(1)}, bf16[128,768]{1,0:T(8,128)(2,1)S(1)}, u32[]{:S(2)}, u32[]{:S(2)}) %collective-permute-start.9) | collective-permute-done | bytes 196640 | tf_op jit(solution)/shard_map/ppermute | solution.py:784
  43.2 9.0 %shard_map.293 = (bf16[1024,1024]{1,0:T(8,128)(2,1)}, f32[1024,384]{1,0:T(8,128)}, bf16[1024,256]{1,0:T(8,128)(2,1)}, bf16[1024,256]{1,0:T(8,128)(2,1)}, bf16[10...) custom-call(s32[1]{0:T(128)} %bitcast.place_ref, s32[8]{0:T(128)} %fusion.22.offset_ref, bf16[256,1024]{1,0:T(8,128)(2,1)} %bitcast.43, ...), custom_call_target="tpu_custom_call" | custom-call | flops 5462499840 | tf_op jit(solution)/shard_map/pallas_call | solution.py:676
  56.1 7.0 %shard_map.295.o0_ref.mixed_ref = bf16[1024,256]{1,0:T(8,128)(2,1)} custom-call(s32[8]{0:T(128)} %slice.147.low_ref, bf16[1024,256]{1,0:T(8,128)(2,1)} %get-tuple-element.157.query_ref, bf16[1024,256]{1,0:T(8,128)(2,1)} %get-tuple-element.158.key_ref, bf16[1024,256]{1,0:T(8,128)(2,1)} %get-tuple-element.159.value_ref, ...), custom_call_target="tpu_custom_call" | custom-call | flops 4024999936 | tf_op jit(solution)/shard_map/pallas_call | solution.py:676
  70.3 3.0 %collective-permute-done.19.o2_ref = bf16[1024,256]{1,0:T(8,128)(2,1)} collective-permute-done((bf16[1024,256]{1,0:T(8,128)(2,1)}, bf16[1024,256]{1,0:T(8,128)(2,1)}, u32[]{:S(2)}, u32[]{:S(2)}) %collective-permute-start.19) | collective-permute-done | bytes 524320 | tf_op jit(solution)/shard_map/ppermute | solution.py:743
  73.3 4.6 %collective-permute-done.17.rest_6_ = bf16[128,2304]{1,0:T(8,128)(2,1)S(1)} collective-permute-done((bf16[128,2304]{1,0:T(8,128)(2,1)}, bf16[128,2304]{1,0:T(8,128)(2,1)S(1)}, u32[]{:S(2)}, u32[]{:S(2)}) %collective-permute-start.17) | collective-permute-done | bytes 589856 | tf_op jit(solution)/shard_map/ppermute | solution.py:784
  86.2 5.1 %shard_map.296 = (bf16[1024,1024]{1,0:T(8,128)(2,1)S(1)}, f32[256,1024]{1,0:T(8,128)S(1)}) custom-call(s32[1]{0:T(128)} %bitcast.place_ref, bf16[256,1024]{1,0:T(8,128)(2,1)S(1)} %bitcast.46, bf16[256,1024]{1,0:T(8,128)(2,1)} %collective-permute-done.x1_ref, bf16[256,1024]{1,0:T(8,128)(2,1)} %collective-permute-done.5.x2_ref, ...), custom_call_target="tpu_custom_call" | custom-call | flops 2875000064 | tf_op jit(solution)/shard_map/pallas_call | solution.py:676
  93.5 3.1 %collective-permute-done.26.rest_7_ = bf16[128,2304]{1,0:T(8,128)(2,1)S(1)} collective-permute-done((bf16[128,2304]{1,0:T(8,128)(2,1)}, bf16[128,2304]{1,0:T(8,128)(2,1)S(1)}, u32[]{:S(2)}, u32[]{:S(2)}) %collective-permute-start.26) | collective-permute-done | bytes 589856 | tf_op jit(solution)/shard_map/ppermute | solution.py:784
  96.6 8.7 %shard_map.297 = (bf16[1024,1152]{1,0:T(8,128)(2,1)S(1)}, bf16[1024,1152]{1,0:T(8,128)(2,1)S(1)}, bf16[1024,1152]{1,0:T(8,128)(2,1)S(1)}) custom-call(s32[8]{0:T(128)S(1)} %copy-done.19, bf16[1024,1024]{1,0:T(8,128)(2,1)S(1)} %get-tuple-element.197.unit_ref, bf16[128,2304]{1,0:T(8,128)(2,1)S(1)} %copy-done.9, ...), custom_call_target="tpu_custom_call" | custom-call | flops 5175000064 | tf_op jit(solution)/shard_map/pallas_call | solution.py:690
  107.4 4.4 %fusion.26 = f32[1152,1024]{1,0:T(8,128)S(1)} fusion(bf16[1024,1152]{1,0:T(8,128)(2,1)S(1)} %get-tuple-element.201.left_ref, bf16[256,1024]{1,0:T(8,128)(2,1)} %collective-permute-done.30, bf16[256,1024]{1,0:T(8,128)(2,1)} %collective-permute-done.10, bf16[256,1024]{1,0:T(8,128)(2,1)} %collective-permute-done.29, bf16[256,1024]{1,0:T(8,128)(2,1)} %bitcast.9), kind=kOutput, calls=%fused_computation.119 | convolution fusion | flops 2424307712 | bytes 9175040 | tf_op jit(solution)/shard_map/dot_general | solution.py:23
  117.9 3.8 %collective-permute-done.33.rest_6_ = bf16[144,1024]{1,0:T(8,128)(2,1)S(1)} collective-permute-done((bf16[144,1024]{1,0:T(8,128)(2,1)S(1)}, bf16[144,1024]{1,0:T(8,128)(2,1)S(1)}, u32[]{:S(2)}, u32[]{:S(2)}) %collective-permute-start.33) | collective-permute-done | bytes 294944 | tf_op jit(solution)/shard_map/ppermute | solution.py:784
  122.6 4.9 %shard_map.298 = (bf16[1024,2304]{1,0:T(8,128)(2,1)S(1)}, bf16[1152,1024]{1,0:T(8,128)(2,1)S(1)}) custom-call(s32[8]{0:T(128)S(1)} %fusion.23.offset_ref, bf16[1024,1024]{1,0:T(8,128)(2,1)S(1)} %pad_maximum_fusion.1.grad_ref, bf16[1024,1152]{1,0:T(8,128)(2,1)S(1)} %get-tuple-element.185.gate_factor_ref, ...), custom_call_target="tpu_custom_call" | custom-call | flops 3104999936 | tf_op jit(solution)/shard_map/pallas_call | solution.py:690
  129.9 9.2 %shard_map.299 = (f32[512,1024]{1,0:T(8,128)S(1)}, bf16[512,1024]{1,0:T(8,128)(2,1)}) custom-call(s32[4]{0:T(128)S(1)} %iota.55.order_ref, s32[8]{0:T(128)S(1)} %copy-done.19, bf16[1024,2304]{1,0:T(8,128)(2,1)S(1)} %get-tuple-element.192.left_ref, bf16[128,2304]{1,0:T(8,128)(2,1)S(1)} %copy-done.9, bf16[128,2304]{1,0:T(8,128)(2,1)} %collective-permute-done.12.rest_1_, ...), custom_call_target="tpu_custom_call" | custom-call | flops 5844113920 | tf_op jit(solution)/shard_map/pallas_call | solution.py:690
  145.4 7.7 %convolution_convert_fusion = bf16[1024,2304]{1,0:T(8,128)(2,1)S(1)} fusion(bf16[1024,1024]{1,0:T(8,128)(2,1)S(1)} %copy-done.25, bf16[1024,2304]{1,0:T(8,128)(2,1)} %copy-done.21), kind=kOutput, calls=%fused_computation | convolution fusion | flops 4834197504 | bytes 11534336 | tf_op jit(solution)/shard_map/dot_general | solution.py:23
  155.3 2.7 collective-permute-done.40
  170.7 4.3 %shard_map.300 = (f32[512,1024]{1,0:T(8,128)S(1)}, bf16[512,1024]{1,0:T(8,128)(2,1)S(1)}) custom-call(s32[4]{0:T(128)S(1)} %iota.56.order_ref, s32[1]{0:T(128)} %constant.399.clone.1.offset_ref, bf16[1024,1152]{1,0:T(8,128)(2,1)S(1)} %copy-done.28, bf16[1152,1024]{1,0:T(8,128)(2,1)S(1)} %copy-done.23), custom_call_target="tpu_custom_call" | custom-call | flops 3065806848 | tf_op jit(solution)/shard_map/pallas_call | solution.py:690
  186.9 3.3 %shard_map.301 = (bf16[1024,256]{1,0:T(8,128)(2,1)S(1)}, f32[512,512]{1,0:T(8,128)S(1)}) custom-call(s32[1]{0:T(128)} %bitcast.place_ref, bf16[256,1024]{1,0:T(8,128)(2,1)} %get-tuple-element.253.g0_ref, bf16[256,1024]{1,0:T(8,128)(2,1)S(1)} %collective-permute-done.47.g1_ref, bf16[256,1024]{1,0:T(8,128)(2,1)S(1)} %collective-permute-done.43.g2_ref, ...), custom_call_target="tpu_custom_call" | custom-call | flops 1724999936 | tf_op jit(solution)/shard_map/pallas_call | solution.py:676
  192.3 15.1 %shard_map.302 = (bf16[1024,512]{1,0:T(8,128)(2,1)S(1)}, f32[8,128]{1,0:T(8,128)S(1)}) custom-call(s32[8]{0:T(128)S(1)} %copy-done.20, bf16[1024,256]{1,0:T(8,128)(2,1)S(1)} %get-tuple-element.211.grad_ref, bf16[1024,256]{1,0:T(8,128)(2,1)S(1)} %copy-done.30, bf16[1024,256]{1,0:T(8,128)(2,1)S(1)} %copy-done.31, bf16[1024,256]{1,0:T(8,128)(2,1)S(1)} %copy-done.32, ...), custom_call_target="tpu_custom_call" | custom-call | flops 8970000384 | tf_op jit(solution)/shard_map/pallas_call | solution.py:676
  214.2 2.7 shard_map.303
  226.7 12.2 %collective-permute-done.52 = bf16[208,512]{1,0:T(8,128)(2,1)S(1)} collective-permute-done((bf16[208,512]{1,0:T(8,128)(2,1)S(1)}, bf16[208,512]{1,0:T(8,128)(2,1)S(1)}, u32[]{:S(2)}, u32[]{:S(2)}) %collective-permute-start.52) | collective-permute-done | bytes 213024 | tf_op jit(solution)/shard_map/ppermute | solution.py:784
  247.9 4.2 %all-to-all-start = ((bf16[4,32,2304]{2,1,0:T(8,128)(2,1)}), bf16[4,32,2304]{2,1,0:T(8,128)(2,1)}, u32[]{:S(2)}, u32[]{:S(2)}) async-start(bf16[4,32,2304]{2,1,0:T(8,128)(2,1)} %bitcast.53), calls=%async_computation | async-start | bytes 1179648 | tf_op jit(solution)/shard_map/all_to_all | solution.py:1203
  262.0 3.0 %shard_map.305 = (f32[32,4608]{1,0:T(8,128)}, f32[32,4608]{1,0:T(8,128)}, f32[1,32]{1,0:T(1,128)}) custom-call(s32[1]{0:T(128)} %bitcast.place_ref, bf16[4,32,2304]{2,1,0:T(8,128)(2,1)} %all-to-all-done.sums_ref, f32[128,4608]{1,0:T(8,128)} %gate_ref.3, f32[128,4608]{1,0:T(8,128)} %up_ref.3, f32[128,1]{1,0:T(8,128)} %copy.39.gain_ref), custom_call_target="tpu_custom_call" | custom-call | flops 1782499968 | tf_op jit(solution)/shard_map/pallas_call | solution.py:626
  (335 shorter events, 139.6 us)
Async XLA Ops:
  6.5 14.0 %collective-permute-start.5 = (bf16[256,1024]{1,0:T(8,128)(2,1)S(1)}, bf16[256,1024]{1,0:T(8,128)(2,1)}, u32[]{:S(2)}, u32[]{:S(2)}) collective-permute-start(bf16[256,1024]{1,0:T(8,128)(2,1)S(1)} %bitcast.44), channel_id=1, source_target_pairs={{0,2},{1,3},{2,0},{3,1},{4,6},{5,7},{6,4},{7,5},{8,10},{9,11},{10,... | collective-permute-start | bytes 1572872 | tf_op jit(solution)/shard_map/ppermute | solution.py:743
  20.5 16.6 %collective-permute-start.10 = (bf16[256,1024]{1,0:T(8,128)(2,1)}, bf16[256,1024]{1,0:T(8,128)(2,1)}, u32[]{:S(2)}, u32[]{:S(2)}) collective-permute-start(bf16[256,1024]{1,0:T(8,128)(2,1)} %bitcast.9), channel_id=1, source_target_pairs={{0,2},{1,3},{2,0},{3,1},{4,6},{5,7},{6,4},{7,5},{8,10},{9,11},{10,... | collective-permute-start | bytes 1572872 | tf_op jit(solution)/shard_map/ppermute | solution.py:743
  22.0 20.4 %collective-permute-start = (bf16[256,1024]{1,0:T(8,128)(2,1)S(1)}, bf16[256,1024]{1,0:T(8,128)(2,1)}, u32[]{:S(2)}, u32[]{:S(2)}) collective-permute-start(bf16[256,1024]{1,0:T(8,128)(2,1)S(1)} %bitcast.45), channel_id=1, source_target_pairs={{0,1},{1,0},{2,3},{3,2},{4,5},{5,4},{6,7},{7,6},{8,9},{9,8},{10,11... | collective-permute-start | bytes 1572872 | tf_op jit(solution)/shard_map/ppermute | solution.py:743
  22.8 19.6 %collective-permute-start.6 = (bf16[256,1024]{1,0:T(8,128)(2,1)}, bf16[256,1024]{1,0:T(8,128)(2,1)S(1)}, u32[]{:S(2)}, u32[]{:S(2)}) collective-permute-start(bf16[256,1024]{1,0:T(8,128)(2,1)} %collective-permute-done.5.x2_ref), channel_id=1, source_target_pairs={{0,1},{1,0},{2,3},{3,2},{4,5},{5,4},{6,7},{7,6},{8,9},{9,8},{10,11... | collective-permute-start | bytes 1572872 | tf_op jit(solution)/shard_map/ppermute | solution.py:743
  37.1 16.3 %collective-permute-start.11 = (bf16[128,2304]{1,0:T(8,128)(2,1)}, bf16[128,2304]{1,0:T(8,128)(2,1)S(1)}, u32[]{:S(2)}, u32[]{:S(2)}) collective-permute-start(bf16[128,2304]{1,0:T(8,128)(2,1)} %shard_map.292.rest_0_), channel_id=1, source_target_pairs={{0,4},{8,0},{16,8},{24,16},{28,24},{20,28},{12,20},{4,12},{1,5},{9... | collective-permute-start | bytes 1769480 | tf_op jit(solution)/shard_map/ppermute | solution.py:784
  38.7 14.7 %collective-permute-start.12 = (bf16[128,2304]{1,0:T(8,128)(2,1)}, bf16[128,2304]{1,0:T(8,128)(2,1)}, u32[]{:S(2)}, u32[]{:S(2)}) collective-permute-start(bf16[128,2304]{1,0:T(8,128)(2,1)} %shard_map.292.rest_0_), channel_id=1, source_target_pairs={{0,8},{8,16},{16,24},{24,28},{28,20},{20,12},{12,4},{4,0},{1,9},{9... | collective-permute-start | bytes 1769480 | tf_op jit(solution)/shard_map/ppermute | solution.py:784
  80.1 16.5 %collective-permute-start.26 = (bf16[128,2304]{1,0:T(8,128)(2,1)}, bf16[128,2304]{1,0:T(8,128)(2,1)S(1)}, u32[]{:S(2)}, u32[]{:S(2)}) collective-permute-start(bf16[128,2304]{1,0:T(8,128)(2,1)} %collective-permute-done.18.rest_5_), channel_id=1, source_target_pairs={{0,8},{8,16},{16,24},{24,28},{28,20},{20,12},{12,4},{4,0},{1,9},{9... | collective-permute-start | bytes 1769480 | tf_op jit(solution)/shard_map/ppermute | solution.py:784
  91.4 13.9 %collective-permute-start.24 = (bf16[144,1024]{1,0:T(8,128)(2,1)S(1)}, bf16[144,1024]{1,0:T(8,128)(2,1)S(1)}, u32[]{:S(2)}, u32[]{:S(2)}) collective-permute-start(bf16[144,1024]{1,0:T(8,128)(2,1)S(1)} %collective-permute-done.23.rest_1_), channel_id=1, source_target_pairs={{0,4},{8,0},{16,8},{24,16},{28,24},{20,28},{12,20},{4,12},{1,5},{9... | collective-permute-start | bytes 884744 | tf_op jit(solution)/shard_map/ppermute | solution.py:784
  92.6 12.7 %collective-permute-start.25 = (bf16[144,1024]{1,0:T(8,128)(2,1)S(1)}, bf16[144,1024]{1,0:T(8,128)(2,1)S(1)}, u32[]{:S(2)}, u32[]{:S(2)}) collective-permute-start(bf16[144,1024]{1,0:T(8,128)(2,1)S(1)} %dynamic-slice_convert_fusion.1.rest_0_), channel_id=1, source_target_pairs={{0,8},{8,16},{16,24},{24,28},{28,20},{20,12},{12,4},{4,0},{1,9},{9... | collective-permute-start | bytes 884744 | tf_op jit(solution)/shard_map/ppermute | solution.py:784
  144.0 14.0 %collective-permute-start.40 = (bf16[256,1024]{1,0:T(8,128)(2,1)S(1)}, bf16[256,1024]{1,0:T(8,128)(2,1)S(1)}, u32[]{:S(2)}, u32[]{:S(2)}) collective-permute-start(bf16[256,1024]{1,0:T(8,128)(2,1)S(1)} %add_convert_fusion.8), channel_id=1, source_target_pairs={{0,2},{1,3},{2,0},{3,1},{4,6},{5,7},{6,4},{7,5},{8,10},{9,11},{10,... | collective-permute-start | bytes 1572872 | tf_op jit(solution)/shard_map/ppermute | solution.py:743
  162.1 13.3 %collective-permute-start.43 = (bf16[256,1024]{1,0:T(8,128)(2,1)}, bf16[256,1024]{1,0:T(8,128)(2,1)S(1)}, u32[]{:S(2)}, u32[]{:S(2)}) collective-permute-start(bf16[256,1024]{1,0:T(8,128)(2,1)} %get-tuple-element.253.g0_ref), channel_id=1, source_target_pairs={{0,2},{1,3},{2,0},{3,1},{4,6},{5,7},{6,4},{7,5},{8,10},{9,11},{10,... | collective-permute-start | bytes 1572872 | tf_op jit(solution)/shard_map/ppermute | solution.py:743
  163.7 14.4 %collective-permute-start.42 = (bf16[128,2304]{1,0:T(8,128)(2,1)S(1)}, bf16[128,2304]{1,0:T(8,128)(2,1)}, u32[]{:S(2)}, u32[]{:S(2)}) collective-permute-start(bf16[128,2304]{1,0:T(8,128)(2,1)S(1)} %pad_maximum_fusion.3), channel_id=1, source_target_pairs={{0,8},{8,16},{16,24},{24,28},{28,20},{20,12},{12,4},{4,0},{1,9},{9... | collective-permute-start | bytes 1769480 | tf_op jit(solution)/shard_map/ppermute | solution.py:784
  164.1 14.1 %collective-permute-start.41 = (bf16[128,2304]{1,0:T(8,128)(2,1)S(1)}, bf16[128,2304]{1,0:T(8,128)(2,1)}, u32[]{:S(2)}, u32[]{:S(2)}) collective-permute-start(bf16[128,2304]{1,0:T(8,128)(2,1)S(1)} %pad_maximum_fusion.2), channel_id=1, source_target_pairs={{0,4},{8,0},{16,8},{24,16},{28,24},{20,28},{12,20},{4,12},{1,5},{9... | collective-permute-start | bytes 1769480 | tf_op jit(solution)/shard_map/ppermute | solution.py:784
  178.2 13.1 %collective-permute-start.44 = (bf16[512,1024]{1,0:T(8,128)(2,1)S(1)}, bf16[512,1024]{1,0:T(8,128)(2,1)S(1)}, u32[]{:S(2)}, u32[]{:S(2)}) collective-permute-start(bf16[512,1024]{1,0:T(8,128)(2,1)S(1)} %get-tuple-element.206), channel_id=1, source_target_pairs={{0,1},{1,0},{2,3},{3,2},{4,5},{5,4},{6,7},{7,6},{8,9},{9,8},{10,11... | collective-permute-start | bytes 3145736 | tf_op jit(solution)/shard_map/ppermute | solution.py:743
  184.5 22.9 %collective-permute-start.45 = (bf16[128,2304]{1,0:T(8,128)(2,1)S(1)}, bf16[128,2304]{1,0:T(8,128)(2,1)S(1)}, u32[]{:S(2)}, u32[]{:S(2)}) collective-permute-start(bf16[128,2304]{1,0:T(8,128)(2,1)S(1)} %get-tuple-element.264), channel_id=1, source_target_pairs={{0,4},{8,0},{16,8},{24,16},{28,24},{20,28},{12,20},{4,12},{1,5},{9... | collective-permute-start | bytes 1769480 | tf_op jit(solution)/shard_map/ppermute | solution.py:784
  186.4 21.0 %collective-permute-start.46 = (bf16[128,2304]{1,0:T(8,128)(2,1)S(1)}, bf16[128,2304]{1,0:T(8,128)(2,1)S(1)}, u32[]{:S(2)}, u32[]{:S(2)}) collective-permute-start(bf16[128,2304]{1,0:T(8,128)(2,1)S(1)} %get-tuple-element.263), channel_id=1, source_target_pairs={{0,8},{8,16},{16,24},{24,28},{28,20},{20,12},{12,4},{4,0},{1,9},{9... | collective-permute-start | bytes 1769480 | tf_op jit(solution)/shard_map/ppermute | solution.py:784
  191.4 16.0 %collective-permute-start.49 = (bf16[256,1024]{1,0:T(8,128)(2,1)S(1)}, bf16[256,1024]{1,0:T(8,128)(2,1)S(1)}, u32[]{:S(2)}, u32[]{:S(2)}) collective-permute-start(bf16[256,1024]{1,0:T(8,128)(2,1)S(1)} %add_convert_fusion.7), channel_id=1, source_target_pairs={{0,2},{1,3},{2,0},{3,1},{4,6},{5,7},{6,4},{7,5},{8,10},{9,11},{10,... | collective-permute-start | bytes 1572872 | tf_op jit(solution)/shard_map/ppermute | solution.py:743
  216.9 23.6 %collective-permute-start.51 = (bf16[512,1024]{1,0:T(8,128)(2,1)S(1)}, bf16[512,1024]{1,0:T(8,128)(2,1)S(1)}, u32[]{:S(2)}, u32[]{:S(2)}) collective-permute-start(bf16[512,1024]{1,0:T(8,128)(2,1)S(1)} %get-tuple-element.226), channel_id=1, source_target_pairs={{0,1},{1,0},{2,3},{3,2},{4,5},{5,4},{6,7},{7,6},{8,9},{9,8},{10,11... | collective-permute-start | bytes 3145736 | tf_op jit(solution)/shard_map/ppermute | solution.py:743
  218.6 22.0 %collective-permute-start.63 = (bf16[128,2304]{1,0:T(8,128)(2,1)S(1)}, bf16[128,2304]{1,0:T(8,128)(2,1)S(1)}, u32[]{:S(2)}, u32[]{:S(2)}) collective-permute-start(bf16[128,2304]{1,0:T(8,128)(2,1)S(1)} %get-tuple-element.262), channel_id=1, source_target_pairs={{0,4},{8,0},{16,8},{24,16},{28,24},{20,28},{12,20},{4,12},{1,5},{9... | collective-permute-start | bytes 1769480 | tf_op jit(solution)/shard_map/ppermute | solution.py:784
  220.5 20.0 %collective-permute-start.64 = (bf16[128,2304]{1,0:T(8,128)(2,1)S(1)}, bf16[128,2304]{1,0:T(8,128)(2,1)S(1)}, u32[]{:S(2)}, u32[]{:S(2)}) collective-permute-start(bf16[128,2304]{1,0:T(8,128)(2,1)S(1)} %get-tuple-element.261), channel_id=1, source_target_pairs={{0,8},{8,16},{16,24},{24,28},{28,20},{20,12},{12,4},{4,0},{1,9},{9... | collective-permute-start | bytes 1769480 | tf_op jit(solution)/shard_map/ppermute | solution.py:784
  223.4 15.5 %collective-permute-start.52 = (bf16[208,512]{1,0:T(8,128)(2,1)S(1)}, bf16[208,512]{1,0:T(8,128)(2,1)S(1)}, u32[]{:S(2)}, u32[]{:S(2)}) collective-permute-start(bf16[208,512]{1,0:T(8,128)(2,1)S(1)} %get-tuple-element.276), channel_id=1, source_target_pairs={{0,4},{8,0},{16,8},{24,16},{28,24},{20,28},{12,20},{4,12},{1,5},{9... | collective-permute-start | bytes 638984 | tf_op jit(solution)/shard_map/ppermute | solution.py:784
  225.5 15.0 %collective-permute-start.53 = (bf16[208,512]{1,0:T(8,128)(2,1)S(1)}, bf16[208,512]{1,0:T(8,128)(2,1)S(1)}, u32[]{:S(2)}, u32[]{:S(2)}) collective-permute-start(bf16[208,512]{1,0:T(8,128)(2,1)S(1)} %add_convert_fusion.20), channel_id=1, source_target_pairs={{0,8},{8,16},{16,24},{24,28},{28,20},{20,12},{12,4},{4,0},{1,9},{9... | collective-permute-start | bytes 638984 | tf_op jit(solution)/shard_map/ppermute | solution.py:784
  241.7 13.5 %collective-permute-start.56 = (bf16[256,1024]{1,0:T(8,128)(2,1)}, bf16[256,1024]{1,0:T(8,128)(2,1)S(1)}, u32[]{:S(2)}, u32[]{:S(2)}) collective-permute-start(bf16[256,1024]{1,0:T(8,128)(2,1)} %add_convert_fusion.5), channel_id=1, source_target_pairs={{0,2},{1,3},{2,0},{3,1},{4,6},{5,7},{6,4},{7,5},{8,10},{9,11},{10,... | collective-permute-start | bytes 1572872 | tf_op jit(solution)/shard_map/ppermute | solution.py:743
  247.9 14.0 %all-to-all-start = ((bf16[4,32,2304]{2,1,0:T(8,128)(2,1)}), bf16[4,32,2304]{2,1,0:T(8,128)(2,1)}, u32[]{:S(2)}, u32[]{:S(2)}) async-start(bf16[4,32,2304]{2,1,0:T(8,128)(2,1)} %bitcast.53), calls=%async_computation | async-start | bytes 1179648 | tf_op jit(solution)/shard_map/all_to_all | solution.py:1203
  (105 other events, 910.9 us)
